TPU v7x, 256 devices: a whole 4x4x8 slice. The times are simulated.
256 devices in a mesh: facet: 16 (over z, core), row: 8 (over x_hi, y), sub: 2 (over x_lo).
Axes of the slice: x: 4 (x_hi: 2, x_lo: 2; x = x_hi * 2 + x_lo), y: 4, z: 8, core: 2. Of those that a mesh axis runs over, the one named last changes fastest.
Arguments:
- facet_model: bfloat16 [2, 4, 8192, 8192], P(None, 'sub', ('facet', 'row')), may hold values from -6 to 6
- sub_offsets: int32 [256], replicated, may hold values from 0 to 65535
- tile_rows: int32 [256, 4], P(('facet', 'row', 'sub')), may hold values from 0 to 120
- tile_counts: int32 [256], P(('facet', 'row', 'sub')), may hold values from 1 to 4, as said below
- visibilities: bfloat16 [256, 4, 32, 8, 256], P(('facet', 'row', 'sub')), may hold values from -6 to 6
Outputs:
- residual_facets: bfloat16 [2, 4, 8192, 8192], P(None, 'sub', ('facet', 'row'))
- residual_vis: bfloat16 [256, 4, 32, 8, 256], P(('facet', 'row', 'sub'))
Inputs may be any that keep to these rules, and one draw needn't show every extreme that they name: tile_counts[s] tiles of subgrid s are live, the first ones; some subgrid has all 4 tiles live. Tile j of subgrid s covers subgrid rows tile_rows[s, j] to tile_rows[s, j] + 7; tiles may intersect.
All inputs are finite; a program needn't handle non-finite values.
Results may differ from a plain program's by a relative error of at most 0.014.
Values may be sent and summed in bfloat16 or wider, within the bound.
No kernel may reach another device: no remote copies, remote signals or barrier semaphores. Data moves between devices by JAX's collectives and lax.ppermute only.
A program may use at most 128 MiB of HBM per device.

v0:
```python
import math

import jax
import jax.numpy as jnp
from jax import lax
from jax.sharding import PartitionSpec as P

SKY = 65536
CS = 64
SG = 128


two_pi = 2.0 * math.pi


def modmul(left, right, modulus):
    lower = right % 256
    upper = right // 256
    return (left * lower % modulus + left * upper % modulus * 256) % modulus


def window_taper(pixels):
    places = jnp.arange(pixels, dtype=jnp.float32)
    curve = jnp.sin(math.pi * (places + 0.5) / pixels)
    return 0.25 + 0.75 * curve * curve


def turn_pair(phase_index, modulus):
    angle = phase_index.astype(jnp.float32) * (-two_pi / modulus)
    return (jnp.cos(angle), jnp.sin(angle))


def column_table(facet_ids, pixels, width, modulus, ratio):
    spacing = modulus // pixels
    column_pos = facet_ids // ratio % ratio * pixels
    freqs = spacing * jnp.arange(width, dtype=jnp.int32)
    places = (column_pos[:, None] + jnp.arange(pixels, dtype=jnp.int32)[None, :]) % modulus
    cosine, sine = turn_pair(modmul(freqs[None, :, None], places[:, None, :], modulus), modulus)
    scaled = window_taper(pixels) / math.sqrt(pixels)
    return (jnp.stack([cosine, sine], axis=1) * scaled).astype(jnp.bfloat16)


def row_block(offsets, pixels, width, modulus, count):
    spacing = modulus // pixels
    freqs = (offsets[:, None] + spacing * jnp.arange(width, dtype=jnp.int32)[None, :]) % modulus
    places = jnp.arange(count, dtype=jnp.int32)
    cosine, sine = turn_pair(modmul(freqs[:, :, None], places[None, None, :], modulus), modulus)
    curve = jnp.sin(math.pi * (places.astype(jnp.float32) + 0.5) / pixels)
    scaled = (0.25 + 0.75 * curve * curve) / math.sqrt(pixels)
    return ((jnp.stack([cosine, sine], axis=1) * scaled).astype(jnp.bfloat16), freqs)


def facet_turn(freqs, facet_ids, modulus, pixels, ratio):
    row_pos = facet_ids % ratio * pixels
    return turn_pair(modmul(freqs[:, :, None], row_pos[None, None, :], modulus), modulus)


def grid_table(size):
    places = jnp.arange(size, dtype=jnp.int32)
    angle = (places[:, None] * places[None, :] % size).astype(jnp.float32) * (two_pi / size)
    return (jnp.stack([jnp.cos(angle), jnp.sin(angle)]) / math.sqrt(size)).astype(jnp.bfloat16)


def slot_table(count, ratio):
    facet_ids = jnp.arange(count, dtype=jnp.int32)
    first = facet_ids % ratio
    second = facet_ids // ratio % ratio
    options = jnp.arange(ratio, dtype=jnp.int32)
    hits = (first[:, None, None] == options[None, :, None]) & (
        second[:, None, None] == options[None, None, :]
    )
    return hits.astype(jnp.bfloat16)


def finish_contrib(raw, turn_real, turn_imag):
    part_real = raw[:, 0, :, :, :, 0] - raw[:, 1, :, :, :, 1]
    part_imag = raw[:, 0, :, :, :, 1] + raw[:, 1, :, :, :, 0]
    real_turn = turn_real[:, :, :, None, None]
    imag_turn = turn_imag[:, :, :, None, None]
    out_real = real_turn * part_real - imag_turn * part_imag
    out_imag = real_turn * part_imag + imag_turn * part_real
    joined = jnp.stack([out_real, out_imag], axis=4)
    return jnp.transpose(joined, (0, 2, 3, 1, 4, 5)).astype(jnp.bfloat16)


def assemble(contrib, slots, grid):
    width = contrib.shape[2]
    terms = contrib.shape[1]
    ratio = slots.shape[1]
    size = width * ratio
    placed = jnp.einsum("fab,ftkcl->katclb", slots, contrib, preferred_element_type=jnp.float32)
    amatrix = placed.reshape(size, terms, 2, size).astype(jnp.bfloat16)
    first = jnp.einsum("zum,mtcn->zutcn", grid, amatrix, preferred_element_type=jnp.float32)
    front = jnp.stack(
        [first[0, :, :, 0] - first[1, :, :, 1], first[0, :, :, 1] + first[1, :, :, 0]], axis=2
    ).astype(jnp.bfloat16)
    second = jnp.einsum("utcn,zvn->utczv", front, grid, preferred_element_type=jnp.float32)
    sky_real = second[:, :, 0, 0] - second[:, :, 1, 1]
    sky_imag = second[:, :, 0, 1] + second[:, :, 1, 0]
    return jnp.stack([sky_real, sky_imag], axis=2).astype(jnp.bfloat16)


def degrid_grid(sky_grid, rows, count, observed):
    slots_count, channels, tile_height, span = observed.shape
    size = sky_grid.shape[0]
    nu_values = (jnp.arange(channels, dtype=jnp.float32) + 0.5) / channels - 0.5
    live = jnp.arange(slots_count, dtype=jnp.int32) < count
    target = rows[:, None] + jnp.arange(tile_height, dtype=jnp.int32)[None, :]
    hits = (target[:, :, None] == jnp.arange(size, dtype=jnp.int32)[None, None, :]) & live[
        :, None, None
    ]
    placer = hits.astype(jnp.bfloat16).reshape(slots_count * tile_height, size)
    model_rows = jnp.dot(
        placer, sky_grid.reshape(size, 2 * span), preferred_element_type=jnp.float32
    )
    model_rows = model_rows.reshape(slots_count, tile_height, 2, span)
    model = model_rows[:, None, :, 0] + nu_values[None, :, None, None] * model_rows[:, None, :, 1]
    residual = (observed.astype(jnp.float32) - model) * live[:, None, None, None].astype(
        jnp.float32
    )
    weighted = jnp.stack(
        [jnp.sum(residual, axis=1), jnp.sum(nu_values[None, :, None, None] * residual, axis=1)],
        axis=2,
    )
    weighted = weighted.astype(jnp.bfloat16).reshape(slots_count * tile_height, 2 * span)
    regrid = lax.dot_general(
        placer, weighted, (((0,), (0,)), ((), ())), preferred_element_type=jnp.float32
    )
    return (residual.astype(jnp.bfloat16), regrid.reshape(size, 2, 2, size).astype(jnp.bfloat16))


def adjoint_grid(regrid, grid):
    first = jnp.einsum("zum,utcv->zmtcv", grid, regrid, preferred_element_type=jnp.float32)
    back_real = first[0, :, :, 0] + first[1, :, :, 1]
    back_imag = first[0, :, :, 1] - first[1, :, :, 0]
    back_front = jnp.stack([back_real, back_imag], axis=2).astype(jnp.bfloat16)
    second = jnp.einsum("mtcv,zvn->mtczn", back_front, grid, preferred_element_type=jnp.float32)
    grid_real = second[:, :, 0, 0] + second[:, :, 1, 1]
    grid_imag = second[:, :, 1, 0] - second[:, :, 0, 1]
    return jnp.stack([grid_real, grid_imag], axis=2).astype(jnp.bfloat16)


def select_slots(back_grid, slots):
    ratio = slots.shape[1]
    size = back_grid.shape[0]
    width = size // ratio
    terms = back_grid.shape[1]
    shaped = back_grid.reshape(width, ratio, terms, 2, width, ratio)
    return jnp.einsum(
        "fab,katclb->ftkcl", slots, shaped, preferred_element_type=jnp.float32
    ).astype(jnp.bfloat16)


def turn_back(returned, turn_real, turn_imag):
    real_turn = jnp.transpose(turn_real, (0, 2, 1))[:, :, None, :, None]
    imag_turn = jnp.transpose(turn_imag, (0, 2, 1))[:, :, None, :, None]
    part_real = returned[:, :, :, :, 0].astype(jnp.float32)
    part_imag = returned[:, :, :, :, 1].astype(jnp.float32)
    turned = jnp.stack(
        [
            real_turn * part_real + imag_turn * part_imag,
            real_turn * part_imag - imag_turn * part_real,
        ],
        axis=4,
    )
    return turned.astype(jnp.bfloat16)


def paired_terms(turned):
    real_part = turned[:, :, :, :, 0]
    imag_part = turned[:, :, :, :, 1]
    pair_real = jnp.stack([real_part, imag_part], axis=1)
    pair_imag = jnp.stack([imag_part, -real_part], axis=1)
    return jnp.stack([pair_real, pair_imag], axis=5)


def strip_terms(table_part, paired):
    return jnp.einsum("szkp,szftkcl->pftcl", table_part, paired, preferred_element_type=jnp.float32)


def local(facet_model, sub_offsets, tile_rows, tile_counts, visibilities):
    facets_here = facet_model.shape[1]
    pixels = facet_model.shape[3]
    ratio = SG // CS
    pairs = lax.axis_size("sub")
    pair = lax.axis_index("sub")
    strip_group = lax.axis_index(("facet", "row"))
    facet_total = facets_here * pairs
    local_facets = pair * facets_here + jnp.arange(facets_here, dtype=jnp.int32)
    columns = column_table(local_facets, pixels, CS, SKY, ratio)
    strips = jnp.einsum(
        "tfpq,fckq->pftck", facet_model, columns, preferred_element_type=jnp.float32
    ).astype(jnp.bfloat16)
    group_offsets = lax.dynamic_slice_in_dim(sub_offsets, strip_group * pairs, pairs, 0)
    rtable, freqs = row_block(group_offsets, pixels, CS, SKY, pixels)
    turn_real, turn_imag = facet_turn(freqs, local_facets, SKY, pixels, ratio)
    table_part = rtable
    raw = jnp.einsum(
        "szkp,pftcl->szkftcl",
        table_part,
        lax.all_gather(strips, ("facet", "row"), axis=0, tiled=True),
        preferred_element_type=jnp.float32,
    )
    contrib = finish_contrib(raw, turn_real, turn_imag)
    slots = slot_table(facet_total, ratio)
    grid = grid_table(SG)
    sky_grid = assemble(
        lax.all_to_all(contrib, "sub", split_axis=0, concat_axis=1, tiled=True)[0], slots, grid
    )
    residual, regrid = degrid_grid(sky_grid, tile_rows[0], tile_counts[0], visibilities[0])
    back_grid = adjoint_grid(regrid, grid)
    returned = select_slots(back_grid, slots)[None]
    received = lax.all_to_all(returned, "sub", split_axis=1, concat_axis=0, tiled=True)
    turned = turn_back(received, turn_real, turn_imag)
    paired = paired_terms(turned)
    table_part = rtable
    mine = lax.psum_scatter(
        strip_terms(table_part, paired), ("facet", "row"), scatter_dimension=0, tiled=True
    )
    strip_round = mine.astype(jnp.bfloat16)
    residual_facets = jnp.einsum(
        "pftck,fckq->tfpq", strip_round, columns, preferred_element_type=jnp.float32
    ).astype(jnp.bfloat16)
    return (residual_facets, residual[None])


def solution(mesh):
    placed = (
        P(None, "sub", ("facet", "row"), None),
        P(),
        P(("facet", "row", "sub"), None),
        P(("facet", "row", "sub")),
        P(("facet", "row", "sub"), None, None, None, None),
    )
    return jax.shard_map(
        local,
        mesh=mesh,
        in_specs=placed,
        out_specs=(
            P(None, "sub", ("facet", "row"), None),
            P(("facet", "row", "sub"), None, None, None, None),
        ),
        check_vma=False,
    )
```

profile of v0, /device:TPU:1, one launch (start us, length us, event | category | flops | bytes accessed | tf_op | source)
XLA Modules:
  0.0 1007.0 jit_solution(10398024351297575194)
XLA Ops:
  7.2 0.0 all-gather.2.cloned.1.call-start
  7.2 0.1 fusion.98
  7.4 0.4 and_select_fusion.1
  7.8 0.0 copy-start.4
  7.8 19.9 %fusion.28 = (f32[2,1,64,8192]{3,2,1,0:T(8,128)S(1)}, f32[2,1,64,8192]{3,2,1,0:T(8,128)S(1)}) fusion(s32[2,8192]{1,0:T(2,128)S(1)} %get-tuple-element.37, s32[2,8192]{1,0:T(2,128)S(1)} %get-tuple-element.36, s32[64]{0:T(128)S(1)} %iota_multiply_fusion), kind=kLoop, calls=%fused_computation.58 | loop fusion | flops 40894464 | bytes 8519936 | tf_op jit(solution)/shard_map/cos | solution.py:30
  27.7 0.0 copy-start
  27.8 0.0 copy-start.1
  27.8 2.0 copy-done
  29.7 1.3 copy-done.1
  31.1 0.0 copy-done.4
  31.1 2.3 fusion.36
  33.4 0.8 copy.122
  34.1 0.0 all-gather.2.cloned.1.call-update
  34.8 0.1 and.544
  34.9 0.1 and.545
  35.0 0.0 copy-done.3
  35.0 0.1 iota_add_fusion
  35.1 0.1 add.627
  35.2 0.0 copy-done.5
  35.2 0.1 dynamic_slice.3
  35.3 0.1 fusion.101
  35.4 0.3 fusion.104
  35.7 0.1 and_select_fusion.15
  35.8 0.1 fusion.152
  36.0 21.4 %fusion.26 = (f32[2,1,64,8192]{3,2,1,0:T(8,128)}, f32[2,1,64,8192]{3,2,1,0:T(8,128)}) fusion(s32[8192]{0:T(1024)S(1)} %get-tuple-element.44, s32[8192]{0:T(1024)S(1)} %get-tuple-element.45, s32[2,64]{1,0:T(2,128)S(1)} %and_select_fusion.15), kind=kLoop, calls=%fused_computation.56 | loop fusion | flops 40894464 | bytes 8454656 | tf_op jit(solution)/shard_map/cos | solution.py:30
  57.3 132.5 %all-gather.2.cloned.1.call-done = bf16[8192,2,2,2,64]{4,3,2,1,0:T(2,128)(2,1)} async-done(((bf16[64,2,2,2,64]{4,3,2,1,0:T(2,128)(2,1)}), bf16[8192,2,2,2,64]{4,3,2,1,0:T(2,128)(2,1)}) %all-gather.2.cloned.1.call-update) | async-done | bytes 8388624 | tf_op jit(solution)/shard_map/all_gather | solution.py:201
  189.8 10.6 %fusion = f32[2,2,64,2,2,2,64]{6,2,5,4,3,1,0:T(8,128)S(1)} fusion(bf16[8192,2,2,2,64,1,1]{4,3,2,1,0,6,5:T(2,128)(2,1)} %bitcast.270, f32[2,1,64,8192]{3,2,1,0:T(8,128)} %get-tuple-element.29, f32[2,1,64,8192]{3,2,1,0:T(8,128)} %get-tuple-element.28, f32[8192]{0:T(1024)S(1)} %fusion.101), kind=kOutput, calls=%fused_computation.1 | convolution fusion | flops 2153775104 | bytes 17334272 | tf_op jit(solution)/shard_map/szkp,pftcl->szkftcl/dot_general | solution.py:198
  200.4 0.2 subtract_convert_fusion
  200.6 0.1 copy_bitcast_fusion.2
  200.6 0.9 reshape.1156
  201.5 3.4 all-to-all-start
  204.9 3.3 all-to-all-done
  208.2 0.2 reshape.1157
  208.4 0.3 copy.127
  208.7 0.4 fusion.30
  209.2 6.6 copy.128
  215.7 13.1 %reshape.1144 = bf16[128,2,2,128,1]{3,0,2,1,4:T(8,128)(2,1)S(1)} reshape(bf16[64,2,2,2,64,2]{5,4,1,0,3,2:T(8,128)(2,1)} %copy.128) | data formatting | bytes 262144 | tf_op jit(solution)/shard_map/convert_element_type | solution.py:92
  228.8 0.2 fusion.89
  229.1 0.2 fusion.72
  229.4 0.2 fusion.116
  229.6 0.3 fusion.43
  230.1 0.5 fusion.44
  230.6 0.2 fusion.70
  230.9 10.0 add.648
  240.9 3.9 copy.141
  244.8 10.0 sub.140
  254.8 3.9 copy.142
  258.7 0.5 fusion.31
  259.2 0.2 copy.212
  259.4 0.9 reshape.1158
  260.3 3.4 all-to-all-start.1
  263.7 0.0 reduce-scatter.2.cloned.1.call-start
  263.7 0.1 fusion.154
  263.9 3.1 all-to-all-done.1
  267.0 0.2 reshape.1159
  267.3 0.1 fusion.162
  267.4 0.1 fusion.56
  267.6 0.1 maximum_bitcast_fusion.1
  267.7 16.6 %convolution_bitcast_fusion = f32[8192,2,2,2,64]{4,0,3,2,1:T(8,128)} fusion(bf16[2,2,2,2,64,1,64]{6,4,1,0,5,3,2:T(8,128)(2,1)S(1)} %get-tuple-element.27, bf16[2,2,2,2,64,1,64]{6,4,1,0,5,3,2:T(8,128)(2,1)S(1)} %get-tuple-element.26, f32[2,1,64,8192]{3,2,1,0:T(8,128)} %get-tuple-element.29, f32[2,1,64,8192]{3,2,1,0:T(8,128)} %get-tuple-element.28, ...), kind=kOutput, calls=%fused_computation | convolution fusion | flops 2154299392 | bytes 25460736 | tf_op jit(solution)/shard_map/szkp,szftkcl->pftcl/dot_general | solution.py:178
  284.3 0.0 reduce-scatter.2.cloned.1.call-update
  284.3 1.2 fusion.42
  285.5 707.6 %reduce-scatter.2.cloned.1.call-done = f32[64,2,2,2,64]{4,0,3,2,1:T(8,128)} async-done(((f32[8192,2,2,2,64]{4,0,3,2,1:T(8,128)}), f32[64,2,2,2,64]{4,0,3,2,1:T(8,128)}) %reduce-scatter.2.cloned.1.call-update) | async-done | bytes 131088 | tf_op jit(solution)/shard_map/reduce_scatter | solution.py:217
  993.1 4.8 fusion.3
  997.9 2.3 copy.148
  (30 shorter events, 0.4 us)
Async XLA Ops:
  7.2 182.6 %all-gather.2.cloned.1.call-start = ((), (), s32[]{:S(2)}) async-start(), calls=%async_computation.3 | async-start | bytes 16908288 | tf_op jit(solution)/shard_map/all_gather | solution.py:201
  7.8 23.3 %copy-start.4 = (bf16[2,2,64,8192]{3,2,1,0:T(8,128)(2,1)S(1)}, bf16[2,2,64,8192]{3,2,1,0:T(8,128)(2,1)}, u32[]{:S(2)}) copy-start(bf16[2,2,64,8192]{3,2,1,0:T(8,128)(2,1)} %param.5) | copy-start | bytes 12582916
  27.7 2.0 copy-start
  27.8 3.3 copy-start.1
  31.1 3.9 copy-start.3
  31.1 4.1 copy-start.5
  201.5 6.7 all-to-all-start
  215.7 13.9 %copy-start.2 = (bf16[1,4,32,8,256]{4,3,2,1,0:T(8,128)(2,1)S(1)}, bf16[1,4,32,8,256]{4,3,2,1,0:T(8,128)(2,1)}, u32[]{:S(2)}) copy-start(bf16[1,4,32,8,256]{4,3,2,1,0:T(8,128)(2,1)} %param.9) | copy-start | bytes 1572868
  260.3 6.7 all-to-all-start.1
  263.7 729.5 %reduce-scatter.2.cloned.1.call-start = ((), (), s32[]{:S(2)}) async-start(), calls=%async_computation.4 | async-start | bytes 33816576 | tf_op jit(solution)/shard_map/reduce_scatter | solution.py:217
Sparse Core Ops, SparseCore 0:
  34.3 155.4 all-gather.1
  284.5 708.6 reduce-scatter.1
where the time goes:
time: 1020 us; the launch traced here: 1010 us
  waiting for transfers between devices  847 us (83%)
  local copies, waits for them, and re-layouts  57 us (6%)
  other arithmetic  45 us (4%)
  matrix products  36.5 us (4%)
  between operations  15.1 us (1%)
    reduce_scatter x1, waiting for transfers between devices, local(): lax.psum_scatter(strip_terms(table_part, paired), ('facet', 'row'), scatt...  708 us
    all_gather x1, waiting for transfers between devices, local(): lax.all_gather(strips, ('facet', 'row'), axis=0, tiled=True)  132 us
    cos x4, other arithmetic, turn_pair(): return (jnp.cos(angle), jnp.sin(angle))  41.6 us
  transfers between devices with their start and end apart: 4, of which 4 were waited for; matrix products, arithmetic and copies ran while one was open for 2% of the time, Pallas kernels for 0%

commit v1 on v0

v1 whole, which is shorter than its diff:
```python
import math

import jax
import jax.numpy as jnp
from jax import lax
from jax.experimental import pallas as pl
from jax.experimental.pallas import tpu as pltpu
from jax.sharding import Mesh
from jax.sharding import PartitionSpec as P

SKY = 65536
FP = 8192
CS = 64
SG = 128
TM = 4
TR = 8
CH = 32
W = TM * TR
PB = 64
ROWS = 8
LP = ROWS * PB
LS = 32
QT = 1024

f32 = jnp.float32
bf16 = jnp.bfloat16


def turn(index, period):
    quarter = period // 4
    quadrant = (index + quarter // 2) // quarter
    x = (index - quadrant * quarter).astype(f32) * (2.0 * math.pi / period)
    y = x * x
    sine = x * (1.0 + y * (-1.0 / 6 + y * (1.0 / 120 + y * (-1.0 / 5040 + y * (1.0 / 362880)))))
    cosine = 1.0 + y * (-0.5 + y * (1.0 / 24 + y * (-1.0 / 720 + y * (1.0 / 40320 - y * (1.0 / 3628800)))))
    swap = (quadrant & 1) == 1
    first = jnp.where(swap, sine, cosine)
    second = jnp.where(swap, cosine, sine)
    first = jnp.where((quadrant == 1) | (quadrant == 2), -first, first)
    second = jnp.where((quadrant & 3) >= 2, -second, second)
    return first, second


def taper(place):
    cosine, _ = turn(2 * place + 1, 2 * FP)
    return 0.625 - 0.375 * cosine


def iota(shape, dim):
    return lax.broadcasted_iota(jnp.int32, shape, dim)


def strips_kernel(model_ref, out_ref, table_ref, acc_ref):
    step = pl.program_id(0)
    place = step * QT + iota((8, QT), 1)
    line = iota((8, QT), 0)
    scale = taper(place) * (1.0 / math.sqrt(FP))
    low_re, low_im = turn((line * place) & (FP - 1), FP)
    low_re, low_im = low_re * scale, low_im * scale
    high_re, high_im = turn((8 * line * place) & (FP - 1), FP)
    real, imag = [], []
    for k in range(8):
        re, im = high_re[k : k + 1], high_im[k : k + 1]
        real.append(low_re * re - low_im * im)
        imag.append(-(low_re * im + low_im * re))
    table = jnp.concatenate(real + imag, axis=0).astype(bf16)
    table_ref[...] = table
    model = model_ref[...].reshape(4 * PB, QT)
    part = lax.dot_general(model, table, (((1,), (1,)), ((), ())), preferred_element_type=f32)

    @pl.when(step == 0)
    def _():
        acc_ref[...] = part

    @pl.when(step > 0)
    def _():
        acc_ref[...] += part

    @pl.when(step == FP // QT - 1)
    def _():
        parts = []
        for a in range(2):
            for t in range(2):
                at = (t * 2 + a) * PB
                parts.append(acc_ref[at : at + PB, :])
        strip = jnp.concatenate(parts, axis=1).astype(bf16)
        for r in range(ROWS):
            out_ref[r] = strip


def strips_call(model):
    return pl.pallas_call(
        strips_kernel,
        grid=(FP // QT,),
        in_specs=[pl.BlockSpec((2, 2, PB, QT), lambda i: (0, 0, 0, i))],
        out_specs=[
            pl.BlockSpec((ROWS, PB, 8 * CS), lambda i: (0, 0, 0)),
            pl.BlockSpec((2 * CS, QT), lambda i: (0, i)),
        ],
        out_shape=[
            jax.ShapeDtypeStruct((ROWS, PB, 8 * CS), bf16),
            jax.ShapeDtypeStruct((2 * CS, FP), bf16),
        ],
        scratch_shapes=[pltpu.VMEM((4 * PB, 2 * CS), f32)],
        cost_estimate=pl.CostEstimate(flops=2 * 256 * 128 * FP, bytes_accessed=7 << 20, transcendentals=0),
        name="strips",
    )(model)


def operator_kernel(offsets_ref, tiles_ref, where_ref, h_ref, tre_ref, tim_ref, d_ref, e_ref):
    step = pl.program_id(0)
    core, row, base = where_ref[0], where_ref[1], where_ref[2]

    @pl.when(step == 0)
    def _():
        u = iota((SG, LP), 0)
        p = base + iota((SG, LP), 1)
        n = (SG * u - p) & (FP - 1)
        _, under = turn(n, 2 * FP)
        _, over = turn((CS * n) & (2 * FP - 1), 2 * FP)
        ratio = jnp.where(n == 0, float(CS), over / jnp.where(n == 0, 1.0, under))
        ratio = ratio * taper(p) * (1.0 / 1024)
        re, im = turn(((CS - 1) * n) & (2 * FP - 1), 2 * FP)
        re, im = re * ratio, im * ratio
        cu, su = turn(u, SG)
        for i, part in enumerate((re, im, re * cu - im * su, re * su + im * cu)):
            for q in range(LP // 128):
                d_ref[i, q] = part[:, q * 128 : (q + 1) * 128]

    lane = iota((8, LP), 1) + base
    line = iota((8, LP), 0)
    offset = jnp.zeros((8, LP), jnp.int32)
    index = []
    for i in range(4):
        g = step * 4 + i
        o, z, b = g // 16, (g // 2) % 8, g % 2
        c = core + o - 2 * core * o
        facet = z * 2 + c
        index.append(facet * 2 + b)
        off = offsets_ref[2 * (facet * ROWS + row) + b]
        offset = jnp.where((line & 3) == i, off, offset)
    place = lane + jnp.where(line >= 4, FP, 0)
    cosine, sine = turn((offset * place) & (SKY - 1), SKY)
    e_ref[0] = cosine
    e_ref[1] = -sine
    blocks = [[] for _ in range(4)]
    for i in range(4):
        for j in range(TM):
            at = tiles_ref[index[i] * TM + j]
            for a in range(2):
                er = e_ref[0, a * 4 + i : a * 4 + i + 1, :]
                ei = e_ref[1, a * 4 + i : a * 4 + i + 1, :]
                dr = jnp.concatenate([d_ref[2 * a, q, pl.ds(at, TR), :] for q in range(LP // 128)], axis=1)
                di = jnp.concatenate([d_ref[2 * a + 1, q, pl.ds(at, TR), :] for q in range(LP // 128)], axis=1)
                blocks[2 * a].append(dr * er - di * ei)
                blocks[2 * a + 1].append(dr * ei + di * er)
    for a in range(2):
        for c in range(2):
            block = jnp.concatenate(blocks[2 * a + c], axis=0)
            h_ref[:, (2 * a + c) * LP : (2 * a + c + 1) * LP] = block.astype(bf16)
            out = tre_ref if c == 0 else tim_ref
            out[a * LP : (a + 1) * LP, :] = block.T.astype(bf16)


def operator_call(offsets, tiles, where):
    smem = pl.BlockSpec(memory_space=pltpu.SMEM)
    return pl.pallas_call(
        operator_kernel,
        grid=(LS // 4,),
        in_specs=[smem, smem, smem],
        out_specs=[
            pl.BlockSpec((4 * W, 4 * LP), lambda i: (i, 0)),
            pl.BlockSpec((2 * LP, 4 * W), lambda i: (0, i)),
            pl.BlockSpec((2 * LP, 4 * W), lambda i: (0, i)),
        ],
        out_shape=[
            jax.ShapeDtypeStruct((LS * W, 4 * LP), bf16),
            jax.ShapeDtypeStruct((2 * LP, LS * W), bf16),
            jax.ShapeDtypeStruct((2 * LP, LS * W), bf16),
        ],
        scratch_shapes=[pltpu.VMEM((4, LP // 128, SG, 128), f32), pltpu.VMEM((2, 8, LP), f32)],
        cost_estimate=pl.CostEstimate(flops=20 << 20, bytes_accessed=8 << 20, transcendentals=0),
        name="operator",
    )(offsets, tiles, where)


def cross(x, sign):
    rows, lanes = x.shape
    left = iota((rows, 2 * CS), 1) < CS
    parts = []
    for at in range(0, lanes, 2 * CS):
        turned = pltpu.roll(x[:, at : at + 2 * CS].astype(f32), CS, 1)
        parts.append(jnp.where(left, -sign * turned, sign * turned).astype(bf16))
    return jnp.concatenate(parts, axis=1)


def fore_kernel(h_ref, strips_ref, own_ref, other_ref, rhs_ref):
    step = pl.program_id(0)

    @pl.when(step == 0)
    def _():
        strips = strips_ref[...].reshape(LP, 8 * CS)
        crossed = cross(strips, 1.0)
        for a in range(2):
            rhs_ref[2 * a * LP : (2 * a + 1) * LP, :] = strips[:, a * 4 * CS : (a + 1) * 4 * CS]
            rhs_ref[(2 * a + 1) * LP : (2 * a + 2) * LP, :] = crossed[:, a * 4 * CS : (a + 1) * 4 * CS]

    out = jnp.dot(h_ref[...], rhs_ref[...], preferred_element_type=f32)
    out = out.reshape(8, W, 4 * CS).astype(bf16)

    @pl.when(step < 2)
    def _():
        own_ref[...] = out

    @pl.when(step >= 2)
    def _():
        other_ref[...] = out


def fore_call(h, strips):
    return pl.pallas_call(
        fore_kernel,
        grid=(4,),
        in_specs=[
            pl.BlockSpec((8 * W, 4 * LP), lambda i: (i, 0)),
            pl.BlockSpec((ROWS, PB, 8 * CS), lambda i: (0, 0, 0)),
        ],
        out_specs=[
            pl.BlockSpec((8, W, 4 * CS), lambda i: (jnp.minimum(i, 1), 0, 0)),
            pl.BlockSpec((8, W, 4 * CS), lambda i: (jnp.maximum(i, 2) - 2, 0, 0)),
        ],
        out_shape=[jax.ShapeDtypeStruct((LS // 2, W, 4 * CS), bf16)] * 2,
        scratch_shapes=[pltpu.VMEM((4 * LP, 4 * CS), bf16)],
        cost_estimate=pl.CostEstimate(flops=2 << 30, bytes_accessed=5 << 20, transcendentals=0),
        name="fore",
    )(h, strips)


def subgrid_kernel(count_ref, parts_ref, vis_ref, res_ref, out_ref):
    l = iota((2 * CS, SG), 0) & (CS - 1)
    upper = iota((2 * CS, SG), 0) < CS
    v = iota((2 * CS, SG), 1)
    rows = []
    for b in range(2):
        cosine, sine = turn((v * (2 * l + b)) & (SG - 1), SG)
        real = jnp.where(upper, cosine, -sine)
        imag = jnp.where(upper, sine, cosine)
        rows.append(jnp.concatenate([real, imag], axis=1))
    table = (jnp.concatenate(rows, axis=0) * (1.0 / math.sqrt(SG))).astype(bf16)

    fronts = []
    for b in range(2):
        total = parts_ref[b].astype(f32)
        for z in range(1, 8):
            total = total + parts_ref[2 * z + b].astype(f32)
        fronts.append(total.astype(bf16))
    front = jnp.concatenate(
        [jnp.concatenate([fronts[b][:, t * 2 * CS : (t + 1) * 2 * CS] for b in range(2)], axis=1) for t in range(2)],
        axis=0,
    )
    sky = jnp.dot(front, table, preferred_element_type=f32).astype(bf16).astype(f32)
    count = count_ref[0]
    weighted = [[], []]
    for j in range(TM):
        m0 = sky[j * TR : (j + 1) * TR]
        m1 = sky[W + j * TR : W + (j + 1) * TR]
        live = jnp.where(j < count, 1.0, 0.0)
        w0 = jnp.zeros((TR, 2 * SG), f32)
        w1 = jnp.zeros((TR, 2 * SG), f32)
        for c in range(CH):
            nu = (c + 0.5) / CH - 0.5
            res = (vis_ref[j, c].astype(f32) - (m0 + nu * m1)) * live
            res_ref[j, c] = res.astype(bf16)
            w0 = w0 + res
            w1 = w1 + nu * res
        weighted[0].append(w0)
        weighted[1].append(w1)
    weight = jnp.concatenate(weighted[0] + weighted[1], axis=0).astype(bf16)
    back = lax.dot_general(weight, table, (((1,), (1,)), ((), ())), preferred_element_type=f32).astype(bf16)
    for b in range(2):
        block = jnp.concatenate([back[t * W : (t + 1) * W, b * 2 * CS : (b + 1) * 2 * CS] for t in range(2)], axis=1)
        for z in range(8):
            out_ref[2 * z + b] = block


def subgrid_call(count, parts, vis):
    return pl.pallas_call(
        subgrid_kernel,
        in_specs=[
            pl.BlockSpec(memory_space=pltpu.SMEM),
            pl.BlockSpec(memory_space=pltpu.VMEM),
            pl.BlockSpec(memory_space=pltpu.VMEM),
        ],
        out_specs=[pl.BlockSpec(memory_space=pltpu.VMEM)] * 2,
        out_shape=[
            jax.ShapeDtypeStruct((TM, CH, TR, 2 * SG), bf16),
            jax.ShapeDtypeStruct((LS // 2, W, 4 * CS), bf16),
        ],
        cost_estimate=pl.CostEstimate(flops=20 << 20, bytes_accessed=2 << 20, transcendentals=0),
        name="subgrid",
    )(count, parts, vis)


def back_kernel(tre_ref, tim_ref, own_ref, other_ref, out_ref, rhs_ref):
    step = pl.program_id(0)
    half = LS * W // 2

    @pl.when(step == 0)
    def _():
        for o, ref in enumerate((own_ref, other_ref)):
            rows = ref[...].reshape(half, 4 * CS)
            rhs_ref[o * half : (o + 1) * half, :] = rows
            rhs_ref[(2 + o) * half : (3 + o) * half, :] = cross(rows, -1.0)

    out = jnp.dot(tre_ref[...], rhs_ref[: 2 * half], preferred_element_type=f32)
    out = out + jnp.dot(tim_ref[...], rhs_ref[2 * half :], preferred_element_type=f32)
    out_ref[...] = out.reshape(4, PB, 4 * CS).astype(bf16)


def back_call(tre, tim, own, other):
    whole = pl.BlockSpec((LS // 2, W, 4 * CS), lambda i: (0, 0, 0))
    return pl.pallas_call(
        back_kernel,
        grid=(4,),
        in_specs=[
            pl.BlockSpec((4 * PB, LS * W), lambda i: (i, 0)),
            pl.BlockSpec((4 * PB, LS * W), lambda i: (i, 0)),
            whole,
            whole,
        ],
        out_specs=pl.BlockSpec((4, PB, 4 * CS), lambda i: (i % 2, 0, i // 2)),
        out_shape=jax.ShapeDtypeStruct((ROWS, PB, 8 * CS), bf16),
        scratch_shapes=[pltpu.VMEM((2 * LS * W, 4 * CS), bf16)],
        cost_estimate=pl.CostEstimate(flops=2 << 30, bytes_accessed=6 << 20, transcendentals=0),
        name="back",
    )(tre, tim, own, other)


def facets_kernel(parts_ref, table_ref, out_ref, lhs_ref):
    @pl.when(pl.program_id(0) == 0)
    def _():
        total = parts_ref[0].astype(f32)
        for r in range(1, ROWS):
            total = total + parts_ref[r].astype(f32)
        total = total.astype(bf16)
        for a in range(2):
            for t in range(2):
                at = (a * 2 + t) * 2 * CS
                lhs_ref[(t * 2 + a) * PB : (t * 2 + a + 1) * PB, :] = total[:, at : at + 2 * CS]

    out = jnp.dot(lhs_ref[...], table_ref[...], preferred_element_type=f32)
    out_ref[...] = out.reshape(2, 2, PB, QT).astype(bf16)


def facets_call(parts, table):
    return pl.pallas_call(
        facets_kernel,
        grid=(FP // QT,),
        in_specs=[
            pl.BlockSpec((ROWS, PB, 8 * CS), lambda i: (0, 0, 0)),
            pl.BlockSpec((2 * CS, QT), lambda i: (0, i)),
        ],
        out_specs=pl.BlockSpec((2, 2, PB, QT), lambda i: (0, 0, 0, i)),
        out_shape=jax.ShapeDtypeStruct((2, 2, PB, FP), bf16),
        scratch_shapes=[pltpu.VMEM((4 * PB, 2 * CS), bf16)],
        cost_estimate=pl.CostEstimate(flops=2 * 256 * 128 * FP, bytes_accessed=7 << 20, transcendentals=0),
        name="facets",
    )(parts, table)


def local(facet_model, sub_offsets, tile_rows, tile_counts, visibilities):
    core = lax.axis_index("core")
    row = lax.axis_index("row")
    facet = lax.axis_index("z") * 2 + core
    where = jnp.stack([core, row, facet * LP]).astype(jnp.int32)

    tiles = lax.all_to_all(
        jnp.broadcast_to(tile_rows, (LS, TM)), ("z", "core", "sub"), split_axis=0, concat_axis=0, tiled=True
    ).reshape(LS * TM)
    strips, table = strips_call(facet_model)
    strips = lax.all_to_all(strips, "row", split_axis=0, concat_axis=0, tiled=True)
    h, tre, tim = operator_call(sub_offsets, tiles, where)

    swap = [(0, 1), (1, 0)]
    own, other = fore_call(h, strips)
    other = lax.ppermute(other, "core", swap)
    parts = (own.astype(f32) + other.astype(f32)).astype(bf16)
    parts = lax.all_to_all(parts, ("z", "sub"), split_axis=0, concat_axis=0, tiled=True)
    residual, back = subgrid_call(tile_counts, parts, visibilities[0])
    own = lax.all_to_all(back, ("z", "sub"), split_axis=0, concat_axis=0, tiled=True)
    other = lax.ppermute(own, "core", swap)
    sums = back_call(tre, tim, own, other)
    sums = lax.all_to_all(sums, "row", split_axis=0, concat_axis=0, tiled=True)
    return facets_call(sums, table), residual[None]


def solution(mesh):
    split = Mesh(mesh.devices.reshape(8, 2, 8, 2), ("z", "core", "row", "sub"))
    whole = ("z", "core", "row", "sub")
    model = P(None, "sub", ("z", "core", "row"), None)
    return jax.shard_map(
        local,
        mesh=split,
        in_specs=(model, P(), P(whole, None), P(whole), P(whole, None, None, None, None)),
        out_specs=(model, P(whole, None, None, None, None)),
        check_vma=False,
    )
```

time: 1020 us -> 119 us (0.12); the launches traced: 1010 us -> 118 us
  waiting for transfers between devices: 847 us -> 12.9 us
  local copies, waits for them, and re-layouts: 57 us -> 4.59 us
  other arithmetic: 45 us -> 3.09 us
  Pallas kernels: 0 us -> 36.6 us
  matrix products: 36.5 us -> 0 us
  blocking collectives: 0 us -> 30.4 us
  starting transfers between devices: 6.84 us -> 29.2 us
  between operations: 15.1 us -> 1.31 us
    reduce_scatter x1 -> x0, waiting for transfers between devices: 708 us -> none  [local(): lax.psum_scatter(strip_terms(table_part, paired), ('facet', 'row'), scatt...]
    all_gather x1 -> x0, waiting for transfers between devices: 132 us -> none  [local(): lax.all_gather(strips, ('facet', 'row'), axis=0, tiled=True)]
    cos x4 -> x0, other arithmetic: 41.6 us -> none  [turn_pair(): return (jnp.cos(angle), jnp.sin(angle))]
    pallas_call x0 -> x6, Pallas kernels: none -> 36.6 us  [the longest x1 8.27 us: operator_call(): pl.pallas_call(operator_kernel, grid=(LS // 4,), in_specs=[smem, smem, sm...]
    dot_general x11 -> x0, matrix products: 36.5 us -> none  [the longest x1 16.6 us: strip_terms(): jnp.einsum('szkp,szftkcl->pftcl', table_part, paired, preferred_element_t...]
    all_to_all x0 -> x2, blocking collectives: none -> 30.4 us  [the longest x1 17.2 us: local(): sums = lax.all_to_all(sums, 'row', split_axis=0, concat_axis=0, tiled=True)]
    convert_element_type x3 -> x0, local copies, waits for them, and re-layouts: 20.5 us -> none  [the longest x2 19.7 us: assemble(): amatrix = placed.reshape(size, terms, 2, size).astype(jnp.bfloat16)]
    all_to_all x2 -> x3, starting transfers between devices: 6.76 us -> 24.4 us  [the longest x1 11 us: local(): lax.all_to_all(jnp.broadcast_to(tile_rows, (LS, TM)), ('z', 'core', 'sub'...]
  transfers between devices with their start and end apart: 4 -> 5, of which waited for: 4 -> 3; matrix products, arithmetic and copies ran while one was open for 2% -> 2% of each run, Pallas kernels for 0% -> 14%
where the time goes in v1:
time: 119 us; the launch traced here: 118 us
  Pallas kernels  36.6 us (31%)
  blocking collectives  30.4 us (26%)
  starting transfers between devices  29.2 us (25%)
  waiting for transfers between devices  12.9 us (11%)
  local copies, waits for them, and re-layouts  4.59 us (4%)
  other arithmetic  3.09 us (3%)
  between operations  1.31 us (1%)
    all_to_all x1, blocking collectives, local(): sums = lax.all_to_all(sums, 'row', split_axis=0, concat_axis=0, tiled=True)  17.2 us
    all_to_all x1, blocking collectives, local(): lax.all_to_all(back, ('z', 'sub'), split_axis=0, concat_axis=0, tiled=True)  13.2 us
    all_to_all x1, starting transfers between devices, local(): lax.all_to_all(jnp.broadcast_to(tile_rows, (LS, TM)), ('z', 'core', 'sub'...  11 us
    all_to_all x1, waiting for transfers between devices, local(): lax.all_to_all(parts, ('z', 'sub'), split_axis=0, concat_axis=0, tiled=True)  10.3 us
    pallas_call x1, Pallas kernels, operator_call(): pl.pallas_call(operator_kernel, grid=(LS // 4,), in_specs=[smem, smem, sm...  8.27 us
    pallas_call x1, Pallas kernels, strips_call(): pl.pallas_call(strips_kernel, grid=(FP // QT,), in_specs=[pl.BlockSpec((2...  8.25 us
    pallas_call x1, Pallas kernels, facets_call(): pl.pallas_call(facets_kernel, grid=(FP // QT,), in_specs=[pl.BlockSpec((R...  7.21 us
    all_to_all x1, starting transfers between devices, local(): lax.all_to_all(parts, ('z', 'sub'), split_axis=0, concat_axis=0, tiled=True)  6.99 us
  transfers between devices with their start and end apart: 5, of which 3 were waited for; matrix products, arithmetic and copies ran while one was open for 2% of the time, Pallas kernels for 14%

profile of v1, /device:TPU:1, one launch (start us, length us, event | category | flops | bytes accessed | tf_op | source)
XLA Modules:
  0.0 118.1 jit_solution(11488518705373951053)
XLA Ops:
  0.6 1.3 %broadcast_in_dim.8 = s32[32,1,4]{2,1,0:T(1,128)} broadcast(s32[4]{0:T(128)} %bitcast.7), dimensions={2} | broadcast | bytes 528 | tf_op jit(solution)/shard_map/broadcast_in_dim | solution.py:378
  1.9 11.0 %all-to-all-start = ((s32[32,1,4]{2,1,0:T(1,128)}), s32[32,1,4]{2,1,0:T(1,128)S(1)}, u32[]{:S(2)}, u32[]{:S(2)}) async-start(s32[32,1,4]{2,1,0:T(1,128)} %broadcast_in_dim.8), calls=%async_computation | async-start | bytes 32768 | tf_op jit(solution)/shard_map/all_to_all | solution.py:377
  12.9 8.3 %strips.1 = (bf16[8,64,512]{2,1,0:T(8,128)(2,1)}, bf16[128,8192]{1,0:T(8,128)(2,1)}) custom-call(bf16[2,2,64,8192]{3,2,1,0:T(8,128)(2,1)} %model_ref.1), custom_call_target="tpu_custom_call" | custom-call | flops 536870912 | bytes 7340032 | tf_op jit(solution)/shard_map/strips/pallas_call | solution.py:92
  21.2 0.0 all-to-all-done
  21.2 6.4 %all-to-all-start.1 = ((bf16[8,64,512]{2,1,0:T(8,128)(2,1)}), bf16[8,64,512]{2,1,0:T(8,128)(2,1)S(1)}, u32[]{:S(2)}, u32[]{:S(2)}) async-start(bf16[8,64,512]{2,1,0:T(8,128)(2,1)} %get-tuple-element.14), calls=%async_computation.1 | async-start | bytes 1048576 | tf_op jit(solution)/shard_map/all_to_all | solution.py:381
  27.6 0.7 pad_add_fusion.where_ref
  28.2 0.5 broadcast.7
  28.7 0.7 reduce.3
  29.4 0.6 reshape.14.tiles_ref
  30.0 8.3 %operator.1 = (bf16[1024,2048]{1,0:T(8,128)(2,1)}, bf16[1024,1024]{1,0:T(8,128)(2,1)}, bf16[1024,1024]{1,0:T(8,128)(2,1)}) custom-call(s32[256]{0:T(256)} %offsets_ref.1, s32[128]{0:T(128)} %reshape.14.tiles_ref, s32[3]{0:T(128)} %pad_add_fusion.where_ref), custom_call_target="tpu_custom_call" | custom-call | flops 20971520 | bytes 8388608 | tf_op jit(solution)/shard_map/operator/pallas_call | solution.py:167
  38.3 0.0 all-to-all-done.1.strips_ref
  38.3 0.0 copy-start.1
  38.3 0.8 copy-done.1
  39.1 5.1 %fore.1 = (bf16[16,32,256]{2,1,0:T(8,128)(2,1)}, bf16[16,32,256]{2,1,0:T(8,128)(2,1)}) custom-call(bf16[1024,2048]{1,0:T(8,128)(2,1)} %get-tuple-element.13.h_ref, bf16[8,64,512]{2,1,0:T(8,128)(2,1)} %copy-done.1), custom_call_target="tpu_custom_call" | custom-call | flops 2147483648 | bytes 5242880 | tf_op jit(solution)/shard_map/fore/pallas_call | solution.py:221
  44.2 1.1 collective-permute-start
  45.3 1.4 %collective-permute-done = bf16[16,32,256]{2,1,0:T(8,128)(2,1)S(1)} collective-permute-done((bf16[16,32,256]{2,1,0:T(8,128)(2,1)}, bf16[16,32,256]{2,1,0:T(8,128)(2,1)S(1)}, u32[]{:S(2)}, u32[]{:S(2)}) %collective-permute-start) | collective-permute-done | bytes 262176 | tf_op jit(solution)/shard_map/ppermute | solution.py:386
  46.7 1.7 %add_convert_fusion = bf16[16,32,256]{2,1,0:T(8,128)(2,1)} fusion(bf16[16,32,256]{2,1,0:T(8,128)(2,1)S(1)} %collective-permute-done, bf16[16,32,256]{2,1,0:T(8,128)(2,1)} %get-tuple-element.15), kind=kLoop, calls=%fused_computation | loop fusion | flops 524288 | bytes 786432 | tf_op jit(solution)/shard_map/convert_element_type | solution.py:387
  48.5 7.0 %all-to-all-start.2 = ((bf16[16,32,256]{2,1,0:T(8,128)(2,1)}), bf16[16,32,256]{2,1,0:T(8,128)(2,1)S(1)}, u32[]{:S(2)}, u32[]{:S(2)}) async-start(bf16[16,32,256]{2,1,0:T(8,128)(2,1)} %add_convert_fusion), calls=%async_computation.2 | async-start | bytes 524288 | tf_op jit(solution)/shard_map/all_to_all | solution.py:388
  56.1 10.3 %all-to-all-done.2.parts_ref = bf16[16,32,256]{2,1,0:T(8,128)(2,1)S(1)} async-done(((bf16[16,32,256]{2,1,0:T(8,128)(2,1)}), bf16[16,32,256]{2,1,0:T(8,128)(2,1)S(1)}, u32[]{:S(2)}, u32[]{:S(2)}) %all-to-all-start.2) | async-done | bytes 262176 | tf_op jit(solution)/shard_map/all_to_all | solution.py:388
  66.4 0.0 copy-start
  66.4 0.7 copy-done
  67.1 2.7 %subgrid.1 = (bf16[4,32,8,256]{3,2,1,0:T(8,128)(2,1)}, bf16[16,32,256]{2,1,0:T(8,128)(2,1)}) custom-call(s32[1]{0:T(128)S(6)} %copy.7.count_ref, bf16[16,32,256]{2,1,0:T(8,128)(2,1)} %copy-done, bf16[4,32,8,256]{3,2,1,0:T(8,128)(2,1)} %bitcast.6), custom_call_target="tpu_custom_call" | custom-call | flops 20971520 | bytes 2097152 | tf_op jit(solution)/shard_map/subgrid/pallas_call | solution.py:287
  69.8 13.2 %all_to_all.26.own_ref = bf16[16,32,256]{2,1,0:T(8,128)(2,1)S(1)} all-to-all(bf16[16,32,256]{2,1,0:T(8,128)(2,1)} %get-tuple-element.17), channel_id=1, replica_groups=mesh['z'=8,'core'=2,'row'=8,'sub'=2] {'z','sub'}, dimensions={0} | all-to-all | bytes 524288 | tf_op jit(solution)/shard_map/all_to_all | solution.py:390
  83.0 0.0 copy-start.2
  83.0 3.7 %collective-permute-start.1 = (bf16[16,32,256]{2,1,0:T(8,128)(2,1)S(1)}, bf16[16,32,256]{2,1,0:T(8,128)(2,1)S(1)}, u32[]{:S(2)}, u32[]{:S(2)}) collective-permute-start(bf16[16,32,256]{2,1,0:T(8,128)(2,1)S(1)} %all_to_all.26.own_ref), channel_id=1, source_target_pairs={{0,16},{16,0},{1,17},{17,1},{2,18},{18,2},{3,19},{19,3},{4,20},{20... | collective-permute-start | bytes 786440 | tf_op jit(solution)/shard_map/ppermute | solution.py:391
  86.7 1.2 collective-permute-done.1.other_ref
  87.9 0.0 copy-start.3
  87.9 0.0 copy-done.2
  87.9 0.7 copy-done.3
  88.6 5.1 %back.1 = bf16[8,64,512]{2,1,0:T(8,128)(2,1)} custom-call(bf16[1024,1024]{1,0:T(8,128)(2,1)} %get-tuple-element.11.tre_ref, bf16[1024,1024]{1,0:T(8,128)(2,1)} %get-tuple-element.12.tim_ref, bf16[16,32,256]{2,1,0:T(8,128)(2,1)} %copy-done.2, bf16[16,32,256]{2,1,0:T(8,128)(2,1)} %copy-done.3), custom_call_target="tpu_custom_call" | custom-call | flops 2147483648 | bytes 6291456 | tf_op jit(solution)/shard_map/back/pallas_call | solution.py:322
  93.6 17.2 %all_to_all.27.parts_ref = bf16[8,64,512]{2,1,0:T(8,128)(2,1)} all-to-all(bf16[8,64,512]{2,1,0:T(8,128)(2,1)} %back.1), channel_id=1, replica_groups=mesh['z'=8,'core'=2,'row'=8,'sub'=2] {'row'}, dimensions={0} | all-to-all | bytes 1048576 | tf_op jit(solution)/shard_map/all_to_all | solution.py:393
  110.9 7.2 %facets.1 = bf16[2,2,64,8192]{3,2,1,0:T(8,128)(2,1)} custom-call(bf16[8,64,512]{2,1,0:T(8,128)(2,1)} %all_to_all.27.parts_ref, bf16[128,8192]{1,0:T(8,128)(2,1)} %get-tuple-element.18.table_ref), custom_call_target="tpu_custom_call" | custom-call | flops 536870912 | bytes 7340032 | tf_op jit(solution)/shard_map/facets/pallas_call | solution.py:356
Async XLA Ops:
  1.9 19.3 %all-to-all-start = ((s32[32,1,4]{2,1,0:T(1,128)}), s32[32,1,4]{2,1,0:T(1,128)S(1)}, u32[]{:S(2)}, u32[]{:S(2)}) async-start(s32[32,1,4]{2,1,0:T(1,128)} %broadcast_in_dim.8), calls=%async_computation | async-start | bytes 32768 | tf_op jit(solution)/shard_map/all_to_all | solution.py:377
  21.2 17.1 %all-to-all-start.1 = ((bf16[8,64,512]{2,1,0:T(8,128)(2,1)}), bf16[8,64,512]{2,1,0:T(8,128)(2,1)S(1)}, u32[]{:S(2)}, u32[]{:S(2)}) async-start(bf16[8,64,512]{2,1,0:T(8,128)(2,1)} %get-tuple-element.14), calls=%async_computation.1 | async-start | bytes 1048576 | tf_op jit(solution)/shard_map/all_to_all | solution.py:381
  38.3 0.8 copy-start.1
  44.2 2.5 %collective-permute-start = (bf16[16,32,256]{2,1,0:T(8,128)(2,1)}, bf16[16,32,256]{2,1,0:T(8,128)(2,1)S(1)}, u32[]{:S(2)}, u32[]{:S(2)}) collective-permute-start(bf16[16,32,256]{2,1,0:T(8,128)(2,1)} %get-tuple-element.16), channel_id=1, source_target_pairs={{0,16},{16,0},{1,17},{17,1},{2,18},{18,2},{3,19},{19,3},{4,20},{20... | collective-permute-start | bytes 786440 | tf_op jit(solution)/shard_map/ppermute | solution.py:386
  48.5 18.0 %all-to-all-start.2 = ((bf16[16,32,256]{2,1,0:T(8,128)(2,1)}), bf16[16,32,256]{2,1,0:T(8,128)(2,1)S(1)}, u32[]{:S(2)}, u32[]{:S(2)}) async-start(bf16[16,32,256]{2,1,0:T(8,128)(2,1)} %add_convert_fusion), calls=%async_computation.2 | async-start | bytes 524288 | tf_op jit(solution)/shard_map/all_to_all | solution.py:388
  66.4 0.7 copy-start
  83.0 4.9 %copy-start.2 = (bf16[16,32,256]{2,1,0:T(8,128)(2,1)}, bf16[16,32,256]{2,1,0:T(8,128)(2,1)S(1)}, u32[]{:S(2)}) copy-start(bf16[16,32,256]{2,1,0:T(8,128)(2,1)S(1)} %all_to_all.26.own_ref) | copy-start | bytes 786436
  83.0 4.9 %collective-permute-start.1 = (bf16[16,32,256]{2,1,0:T(8,128)(2,1)S(1)}, bf16[16,32,256]{2,1,0:T(8,128)(2,1)S(1)}, u32[]{:S(2)}, u32[]{:S(2)}) collective-permute-start(bf16[16,32,256]{2,1,0:T(8,128)(2,1)S(1)} %all_to_all.26.own_ref), channel_id=1, source_target_pairs={{0,16},{16,0},{1,17},{17,1},{2,18},{18,2},{3,19},{19,3},{4,20},{20... | collective-permute-start | bytes 786440 | tf_op jit(solution)/shard_map/ppermute | solution.py:391
  87.9 0.7 copy-start.3

commit v2 on v1

v2 whole, which is shorter than its diff:
```python
import math

import jax
import jax.numpy as jnp
from jax import lax
from jax.experimental import pallas as pl
from jax.experimental.pallas import tpu as pltpu
from jax.sharding import Mesh
from jax.sharding import PartitionSpec as P

SKY = 65536
FP = 8192
CS = 64
SG = 128
TM = 4
TR = 8
CH = 32
W = TM * TR
PB = 64
ROWS = 8
LP = ROWS * PB
LS = 32
QT = 1024

f32 = jnp.float32
bf16 = jnp.bfloat16


def turn(index, period):
    quarter = period // 4
    quadrant = lax.shift_right_logical(index + quarter // 2, quarter.bit_length() - 1)
    x = (index - quadrant * quarter).astype(f32) * (2.0 * math.pi / period)
    y = x * x
    sine = x * (1.0 + y * (-1.0 / 6 + y * (1.0 / 120 + y * (-1.0 / 5040 + y * (1.0 / 362880)))))
    cosine = 1.0 + y * (-0.5 + y * (1.0 / 24 + y * (-1.0 / 720 + y * (1.0 / 40320 - y * (1.0 / 3628800)))))
    swap = (quadrant & 1) == 1
    first = jnp.where(swap, sine, cosine)
    second = jnp.where(swap, cosine, sine)
    first = jnp.where(((quadrant + 1) & 2) == 2, -first, first)
    second = jnp.where((quadrant & 2) == 2, -second, second)
    return first, second


def taper(place):
    cosine, _ = turn(2 * place + 1, 2 * FP)
    return 0.625 - 0.375 * cosine


def iota(shape, dim):
    return lax.broadcasted_iota(jnp.int32, shape, dim)


def column_start(base_ref):
    place = iota((8, QT), 1)
    line = iota((8, QT), 0)
    tables = turn((line * place) & (QT - 1), QT) + turn((line * place) & (FP - 1), FP) + turn(2 * place + 1, 2 * FP)
    for i, table in enumerate(tables):
        base_ref[i] = table


def column_block(base_ref, step):
    wide = lambda x: jnp.concatenate([x] * (QT // 128), axis=1)
    move_re, move_im = (wide(x) for x in turn((iota((8, 128), 0) * step) & 7, 8))
    tilt_re, tilt_im = (wide(x) for x in turn(jnp.full((8, 128), step, jnp.int32), 8))
    cosine = base_ref[4] * tilt_re - base_ref[5] * tilt_im
    scale = (0.625 - 0.375 * cosine) * (1.0 / math.sqrt(FP))
    low_re = (base_ref[2] * move_re - base_ref[3] * move_im) * scale
    low_im = (base_ref[2] * move_im + base_ref[3] * move_re) * scale
    real, imag = [], []
    for k in range(8):
        re, im = base_ref[0, k : k + 1], base_ref[1, k : k + 1]
        real.append(low_re * re - low_im * im)
        imag.append(-(low_re * im + low_im * re))
    return jnp.concatenate(real + imag, axis=0).astype(bf16)


def subgrid_of(g):
    core = lax.axis_index("core")
    o, z, b = g // 16, (g // 2) % 8, g % 2
    c = core + o - 2 * core * o
    facet = z * 2 + c
    return facet * 2 + b, 2 * (facet * 8 + lax.axis_index("xh") * 4 + lax.axis_index("y")) + b


def line_rows(shape):
    z = lax.axis_index("zh") * 2 + lax.axis_index("zl")
    return (z * 2 + lax.axis_index("core")) * LP + iota(shape, 1)


def phase_table(ref):
    shape = (SG + TR, 2 * CS)
    cosine, sine = turn(iota(shape, 0) & (SG - 1), SG)
    ref[0] = cosine
    ref[1] = jnp.where(iota(shape, 1) < CS, -sine, sine)


def phases(ref, tiles_ref, offsets_ref, first):
    parts = [[], []]
    for i in range(8):
        index, s = subgrid_of(first + i)
        for j in range(TM):
            at = (tiles_ref[index, j] - 16 * offsets_ref[s]) & (SG - 1)
            for c in range(2):
                parts[c].append(ref[c, pl.ds(at, TR), :])
    real, imag = (jnp.concatenate(x, axis=0) for x in parts)
    return jnp.concatenate([real, real], axis=1), jnp.concatenate([imag, imag], axis=1)


def swapped(x):
    return jnp.concatenate([pltpu.roll(x[:, i : i + 2 * CS], CS, 1) for i in range(0, x.shape[1], 2 * CS)], axis=1)


SMEM = pl.BlockSpec(memory_space=pltpu.SMEM)
VMEM = pl.BlockSpec(memory_space=pltpu.VMEM)
HBM = pl.BlockSpec(memory_space=pltpu.HBM)


def params(mib):
    return pltpu.CompilerParams(vmem_limit_bytes=mib << 20)


def strips_kernel(model_ref, out_ref, buffer, sems, base_ref, table_ref):
    rows = PB // 2

    def copy(i):
        return pltpu.make_async_copy(
            model_ref.at[i // 4, (i // 2) % 2, pl.ds((i % 2) * rows, rows), :], buffer.at[i], sems.at[i]
        )

    for i in range(8):
        copy(i).start()
    column_start(base_ref)

    def body(i, carry):
        table_ref[:, pl.ds(pl.multiple_of(i * QT, QT), QT)] = column_block(base_ref, i)
        return carry

    lax.fori_loop(0, FP // QT, body, 0)
    for i in range(8):
        copy(i).wait()
    strips = lax.dot_general(
        buffer[...].reshape(4 * PB, FP), table_ref[...], (((1,), (1,)), ((), ())), preferred_element_type=f32
    ).astype(bf16)
    parts = [strips[(t * 2 + a) * PB : (t * 2 + a + 1) * PB] for a in range(2) for t in range(2)]
    strip = jnp.concatenate(parts, axis=1)
    for r in range(ROWS):
        out_ref[r] = strip


def strips_call(model):
    return pl.pallas_call(
        strips_kernel,
        in_specs=[HBM],
        out_specs=VMEM,
        out_shape=jax.ShapeDtypeStruct((ROWS, PB, 8 * CS), bf16),
        scratch_shapes=[
            pltpu.VMEM((8, PB // 2, FP), bf16),
            pltpu.SemaphoreType.DMA((8,)),
            pltpu.VMEM((6, 8, QT), f32),
            pltpu.VMEM((2 * CS, FP), bf16),
        ],
        compiler_params=params(60),
        cost_estimate=pl.CostEstimate(flops=2 * 256 * 128 * FP, bytes_accessed=5 << 20, transcendentals=0),
        name="strips",
    )(model)


def waves_kernel(d_ref):
    p = line_rows((TR, LP))
    line = iota((TR, LP), 0)

    def body(i, carry):
        n = (SG * (i * TR + line) - p) & (FP - 1)
        _, under = turn(n, 2 * FP)
        _, over = turn((CS * n) & (2 * FP - 1), 2 * FP)
        ratio = jnp.where(n == 0, float(CS), over / jnp.where(n == 0, 1.0, under))
        re, im = turn(((CS - 1) * n) & (2 * FP - 1), 2 * FP)
        for c, part in enumerate((re * ratio, im * ratio)):
            for q in range(LP // 128):
                d_ref[c, q, pl.ds(pl.multiple_of(i * TR, TR), TR), :] = part[:, q * 128 : (q + 1) * 128]
        return carry

    lax.fori_loop(0, SG // TR, body, 0)


def waves_call():
    return pl.pallas_call(
        waves_kernel,
        out_specs=VMEM,
        out_shape=jax.ShapeDtypeStruct((2, LP // 128, SG, 128), f32),
        compiler_params=params(24),
        cost_estimate=pl.CostEstimate(flops=8 << 20, bytes_accessed=1 << 20, transcendentals=0),
        name="waves",
    )()


def operator_kernel(tiles_ref, offsets_ref, count_ref, d_ref, h_ref, live_ref, e_ref):
    live_ref[...] = jnp.where(iota((W, 128), 0) < TR * count_ref[0], 1.0, 0.0)
    place = line_rows((8, LP))
    line = iota((8, LP), 0)
    scale = taper(place) * (1.0 / 1024)

    def body(step, carry):
        offset = jnp.zeros((8, LP), jnp.int32)
        index = []
        for i in range(8):
            at, s = subgrid_of(step * 8 + i)
            index.append(at)
            offset = jnp.where(line == i, offsets_ref[s], offset)
        cosine, sine = turn((offset * place) & (SKY - 1), SKY)
        e_ref[0] = cosine * scale
        e_ref[1] = -sine * scale
        for half in range(2):
            real, imag = [], []
            for i in range(4 * half, 4 * half + 4):
                er = e_ref[0, i : i + 1, :]
                ei = e_ref[1, i : i + 1, :]
                for j in range(TM):
                    at = tiles_ref[index[i], j]
                    dr = jnp.concatenate([d_ref[0, q, pl.ds(at, TR), :] for q in range(LP // 128)], axis=1)
                    di = jnp.concatenate([d_ref[1, q, pl.ds(at, TR), :] for q in range(LP // 128)], axis=1)
                    real.append(dr * er - di * ei)
                    imag.append(dr * ei + di * er)
            rows = pl.ds(pl.multiple_of(step * 8 * W + half * 4 * W, 4 * W), 4 * W)
            h_ref[rows, :LP] = jnp.concatenate(real, axis=0).astype(bf16)
            h_ref[rows, LP:] = jnp.concatenate(imag, axis=0).astype(bf16)
        return carry

    lax.fori_loop(0, LS // 8, body, 0)


def operator_call(tiles, offsets, count, waves):
    return pl.pallas_call(
        operator_kernel,
        in_specs=[SMEM, SMEM, SMEM, VMEM],
        out_specs=[VMEM, VMEM],
        out_shape=[jax.ShapeDtypeStruct((LS * W, 2 * LP), bf16), jax.ShapeDtypeStruct((W, 128), f32)],
        scratch_shapes=[pltpu.VMEM((2, 8, LP), f32)],
        compiler_params=params(24),
        cost_estimate=pl.CostEstimate(flops=20 << 20, bytes_accessed=8 << 20, transcendentals=0),
        name="operator",
    )(tiles, offsets, count, waves)


def fore_kernel(tiles_ref, offsets_ref, h_ref, strips_ref, own_ref, other_ref, rhs_ref, phase_ref):
    phase_table(phase_ref)
    left = iota((PB, 2 * CS), 1) < CS
    for r in range(ROWS):
        strips = strips_ref[r]
        rhs_ref[r * PB : (r + 1) * PB, :] = strips
        for at in range(0, 8 * CS, 2 * CS):
            turned = pltpu.roll(strips[:, at : at + 2 * CS].astype(f32), CS, 1)
            rhs_ref[LP + r * PB : LP + (r + 1) * PB, at : at + 2 * CS] = jnp.where(left, -turned, turned).astype(bf16)
    rows = 8 * W
    for step in range(4):
        out = jnp.dot(h_ref[step * rows : (step + 1) * rows, :], rhs_ref[...], preferred_element_type=f32)
        real, imag = phases(phase_ref, tiles_ref, offsets_ref, step * 8)
        second = out[:, 4 * CS :]
        out = out[:, : 4 * CS] + second * real + swapped(second) * imag
        ref = own_ref if step < 2 else other_ref
        ref[step % 2 * 8 : step % 2 * 8 + 8] = out.reshape(8, W, 4 * CS).astype(bf16)


def fore_call(tiles, offsets, h, strips):
    return pl.pallas_call(
        fore_kernel,
        in_specs=[SMEM, SMEM, VMEM, VMEM],
        out_specs=[VMEM, VMEM],
        out_shape=[jax.ShapeDtypeStruct((LS // 2, W, 4 * CS), bf16)] * 2,
        scratch_shapes=[
            pltpu.VMEM((2 * LP, 8 * CS), bf16),
            pltpu.VMEM((2, SG + TR, 2 * CS), f32),
        ],
        compiler_params=params(24),
        cost_estimate=pl.CostEstimate(flops=1 << 30, bytes_accessed=4 << 20, transcendentals=0),
        name="fore",
    )(tiles, offsets, h, strips)


def add_kernel(own_ref, other_ref, out_ref):
    out_ref[...] = (own_ref[...].astype(f32) + other_ref[...].astype(f32)).astype(bf16)


def add_call(own, other):
    return pl.pallas_call(
        add_kernel,
        in_specs=[VMEM, VMEM],
        out_specs=VMEM,
        out_shape=jax.ShapeDtypeStruct(own.shape, bf16),
        compiler_params=params(24),
        cost_estimate=pl.CostEstimate(flops=1 << 18, bytes_accessed=1 << 20, transcendentals=0),
        name="add",
    )(own, other)


def subgrid_kernel(live_ref, parts_ref, vis_ref, res_ref, out_ref, buffer, sems):
    l = iota((2 * CS, SG), 0) & (CS - 1)
    upper = iota((2 * CS, SG), 0) < CS
    v = iota((2 * CS, SG), 1)
    rows = []
    for b in range(2):
        cosine, sine = turn((v * (2 * l + b)) & (SG - 1), SG)
        real = jnp.where(upper, cosine, -sine)
        imag = jnp.where(upper, sine, cosine)
        rows.append(jnp.concatenate([real, imag], axis=1))
    table = (jnp.concatenate(rows, axis=0) * (1.0 / math.sqrt(SG))).astype(bf16)

    fronts = []
    for b in range(2):
        total = parts_ref[b].astype(f32)
        for z in range(1, 8):
            total = total + parts_ref[2 * z + b].astype(f32)
        fronts.append(total.astype(bf16))
    front = jnp.concatenate(
        [jnp.concatenate([fronts[b][:, t * 2 * CS : (t + 1) * 2 * CS] for b in range(2)], axis=1) for t in range(2)],
        axis=0,
    )
    sky = jnp.dot(front, table, preferred_element_type=f32).astype(bf16).astype(f32)
    weighted = [[], []]
    for j in range(TM):
        m0 = sky[j * TR : (j + 1) * TR]
        m1 = sky[W + j * TR : W + (j + 1) * TR]
        live = live_ref[j * TR : (j + 1) * TR, :]
        live = jnp.concatenate([live, live], axis=1)
        w0 = jnp.zeros((TR, 2 * SG), f32)
        w1 = jnp.zeros((TR, 2 * SG), f32)
        for c in range(CH):
            nu = (c + 0.5) / CH - 0.5
            res = (vis_ref[j, c].astype(f32) - (m0 + nu * m1)) * live
            buffer[j, c] = res.astype(bf16)
            w0 = w0 + res
            w1 = w1 + nu * res
        pltpu.make_async_copy(buffer.at[j], res_ref.at[j], sems.at[j]).start()
        weighted[0].append(w0)
        weighted[1].append(w1)
    weight = jnp.concatenate(weighted[0] + weighted[1], axis=0).astype(bf16)
    back = lax.dot_general(weight, table, (((1,), (1,)), ((), ())), preferred_element_type=f32).astype(bf16)
    for b in range(2):
        block = jnp.concatenate([back[t * W : (t + 1) * W, b * 2 * CS : (b + 1) * 2 * CS] for t in range(2)], axis=1)
        for z in range(8):
            out_ref[2 * z + b] = block
    for j in range(TM):
        pltpu.make_async_copy(buffer.at[j], res_ref.at[j], sems.at[j]).wait()


def subgrid_call(live, parts, vis):
    return pl.pallas_call(
        subgrid_kernel,
        in_specs=[VMEM, VMEM, VMEM],
        out_specs=[HBM, VMEM],
        out_shape=[
            jax.ShapeDtypeStruct((TM, CH, TR, 2 * SG), bf16),
            jax.ShapeDtypeStruct((LS // 2, W, 4 * CS), bf16),
        ],
        scratch_shapes=[pltpu.VMEM((TM, CH, TR, 2 * SG), bf16), pltpu.SemaphoreType.DMA((TM,))],
        compiler_params=params(24),
        cost_estimate=pl.CostEstimate(flops=20 << 20, bytes_accessed=2 << 20, transcendentals=0),
        name="subgrid",
    )(live, parts, vis)


def back_kernel(tiles_ref, offsets_ref, h_ref, own_ref, other_ref, out_ref, rhs_ref, phase_ref):
    phase_table(phase_ref)
    total = LS * W
    left = (iota((8 * W, 8 * CS), 1) & (2 * CS - 1)) < CS
    for step in range(4):
        ref = own_ref if step < 2 else other_ref
        x = ref[step % 2 * 8 : step % 2 * 8 + 8].reshape(8 * W, 4 * CS).astype(f32)
        y = swapped(x)
        real, imag = phases(phase_ref, tiles_ref, offsets_ref, step * 8)
        both = jnp.concatenate([x, x * real - y * imag], axis=1)
        turned = jnp.concatenate([y, y * real + x * imag], axis=1)
        rhs_ref[step * 8 * W : (step + 1) * 8 * W, :] = both.astype(bf16)
        rhs_ref[total + step * 8 * W : total + (step + 1) * 8 * W, :] = jnp.where(left, turned, -turned).astype(bf16)
    dims = (((0,), (0,)), ((), ()))
    for step in range(2):
        at = step * 4 * PB
        out = lax.dot_general(h_ref[:, at : at + 4 * PB], rhs_ref[:total], dims, preferred_element_type=f32)
        out = out + lax.dot_general(h_ref[:, LP + at : LP + at + 4 * PB], rhs_ref[total:], dims, preferred_element_type=f32)
        out_ref[step * 4 : step * 4 + 4] = out.reshape(4, PB, 8 * CS).astype(bf16)


def back_call(tiles, offsets, h, own, other):
    return pl.pallas_call(
        back_kernel,
        in_specs=[SMEM, SMEM, VMEM, VMEM, VMEM],
        out_specs=VMEM,
        out_shape=jax.ShapeDtypeStruct((ROWS, PB, 8 * CS), bf16),
        scratch_shapes=[pltpu.VMEM((2 * LS * W, 8 * CS), bf16), pltpu.VMEM((2, SG + TR, 2 * CS), f32)],
        compiler_params=params(24),
        cost_estimate=pl.CostEstimate(flops=1 << 30, bytes_accessed=4 << 20, transcendentals=0),
        name="back",
    )(tiles, offsets, h, own, other)


def facets_kernel(parts_ref, out_ref, buffer, sems, lhs_ref, base_ref):
    steps = FP // QT
    column_start(base_ref)
    total = parts_ref[0].astype(f32)
    for r in range(1, ROWS):
        total = total + parts_ref[r].astype(f32)
    total = total.astype(bf16)
    for a in range(2):
        for t in range(2):
            at = (a * 2 + t) * 2 * CS
            lhs_ref[(t * 2 + a) * PB : (t * 2 + a + 1) * PB, :] = total[:, at : at + 2 * CS]

    def copy(i):
        return pltpu.make_async_copy(buffer.at[i], out_ref.at[:, :, :, pl.ds(pl.multiple_of(i * QT, QT), QT)], sems.at[i])

    def body(i, carry):
        out = jnp.dot(lhs_ref[...], column_block(base_ref, i), preferred_element_type=f32)
        buffer[i] = out.reshape(2, 2, PB, QT).astype(bf16)
        copy(i).start()
        return carry

    lax.fori_loop(0, steps, body, 0)
    for i in range(steps):
        copy(i).wait()


def facets_call(parts):
    steps = FP // QT
    return pl.pallas_call(
        facets_kernel,
        in_specs=[VMEM],
        out_specs=HBM,
        out_shape=jax.ShapeDtypeStruct((2, 2, PB, FP), bf16),
        scratch_shapes=[
            pltpu.VMEM((steps, 2, 2, PB, QT), bf16),
            pltpu.SemaphoreType.DMA((steps,)),
            pltpu.VMEM((4 * PB, 2 * CS), bf16),
            pltpu.VMEM((6, 8, QT), f32),
        ],
        compiler_params=params(24),
        cost_estimate=pl.CostEstimate(flops=2 * 256 * 128 * FP, bytes_accessed=5 << 20, transcendentals=0),
        name="facets",
    )(parts)


def local(facet_model, sub_offsets, tile_rows, tile_counts, visibilities):
    rows_line, grid_line, all_line = ("xh", "y"), ("zh", "zl", "sub"), ("zh", "zl", "core", "sub")
    swap = [(0, 1), (1, 0)]

    def exchange(x, axes):
        return lax.all_to_all(x, axes, split_axis=0, concat_axis=0, tiled=True)

    tiles = exchange(jnp.broadcast_to(tile_rows, (LS, TM)), all_line)
    strips = exchange(strips_call(facet_model), rows_line)
    h, live = operator_call(tiles, sub_offsets, tile_counts, waves_call())

    own, other = fore_call(tiles, sub_offsets, h, strips)
    other = lax.ppermute(other, "core", swap)
    parts = exchange(add_call(own, other), grid_line)
    residual, back = subgrid_call(live, parts, visibilities[0])
    own = exchange(back, grid_line)
    other = lax.ppermute(own, "core", swap)
    sums = exchange(back_call(tiles, sub_offsets, h, own, other), rows_line)
    return facets_call(sums), residual[None]


def solution(mesh):
    split = Mesh(mesh.devices.reshape(4, 2, 2, 2, 4, 2), ("zh", "zl", "core", "xh", "y", "sub"))
    whole = ("zh", "zl", "core", "xh", "y", "sub")
    model = P(None, "sub", ("zh", "zl", "core", "xh", "y"), None)
    return jax.shard_map(
        local,
        mesh=split,
        in_specs=(model, P(), P(whole, None), P(whole), P(whole, None, None, None, None)),
        out_specs=(model, P(whole, None, None, None, None)),
        check_vma=False,
    )
```

time: 119 us -> 96.3 us (0.81)
  Pallas kernels: 36.6 us -> 18.1 us
  blocking collectives: 30.4 us -> 41.2 us
  starting transfers between devices: 29.2 us -> 23.5 us
  local copies, waits for them, and re-layouts: 4.59 us -> 1.28 us
  other arithmetic: 3.09 us -> 0 us
  waiting for transfers between devices: 12.9 us -> 10.6 us
    pallas_call x6 -> x8, Pallas kernels: 36.6 us -> 18.1 us  [the longest x1 4.27 us: strips_call(): pl.pallas_call(strips_kernel, in_specs=[HBM], out_specs=VMEM, out_shape=j...]
    all_to_all x2 -> x3, blocking collectives: 30.4 us -> 41.2 us  [exchange(): return lax.all_to_all(x, axes, split_axis=0, concat_axis=0, tiled=True)]
    all_to_all x3 -> x2, starting transfers between devices: 24.4 us -> 17.4 us  [exchange(): return lax.all_to_all(x, axes, split_axis=0, concat_axis=0, tiled=True)]
    unnamed x8 -> x4, local copies, waits for them, and re-layouts: 2.2 us -> 0.01 us
    all_to_all x3 -> x2, waiting for transfers between devices: 10.4 us -> 8.23 us  [exchange(): return lax.all_to_all(x, axes, split_axis=0, concat_axis=0, tiled=True)]
    ppermute x1, starting transfers between devices: 1.09 us -> 3.12 us  [local(): other = lax.ppermute(other, 'core', swap)]
    convert_element_type x1 -> x0, other arithmetic: 1.74 us -> none  [local(): parts = (own.astype(f32) + other.astype(f32)).astype(bf16)]
  transfers between devices with their start and end apart: 5 -> 4, of which waited for: 3 -> 4; matrix products, arithmetic and copies ran while one was open for 2% -> 0% of each run, Pallas kernels for 14% -> 8%
where the time goes in v2:
time: 96.3 us; the launch traced here: 96 us
  blocking collectives  41.2 us (43%)
  starting transfers between devices  23.5 us (24%)
  Pallas kernels  18.1 us (19%)
  waiting for transfers between devices  10.6 us (11%)
  between operations  1.36 us (1%)
  local copies, waits for them, and re-layouts  1.28 us (1%)
    all_to_all x3, blocking collectives, exchange(): return lax.all_to_all(x, axes, split_axis=0, concat_axis=0, tiled=True)  41.2 us
    all_to_all x2, starting transfers between devices, exchange(): return lax.all_to_all(x, axes, split_axis=0, concat_axis=0, tiled=True)  17.4 us
    all_to_all x2, waiting for transfers between devices, exchange(): return lax.all_to_all(x, axes, split_axis=0, concat_axis=0, tiled=True)  8.23 us
    pallas_call x1, Pallas kernels, strips_call(): pl.pallas_call(strips_kernel, in_specs=[HBM], out_specs=VMEM, out_shape=j...  4.27 us
    pallas_call x1, Pallas kernels, facets_call(): pl.pallas_call(facets_kernel, in_specs=[VMEM], out_specs=HBM, out_shape=j...  3.88 us
    ppermute x1, starting transfers between devices, local(): other = lax.ppermute(other, 'core', swap)  3.12 us
    ppermute x1, starting transfers between devices, local(): other = lax.ppermute(own, 'core', swap)  2.95 us
    pallas_call x1, Pallas kernels, back_call(): pl.pallas_call(back_kernel, in_specs=[SMEM, SMEM, VMEM, VMEM, VMEM], out_...  2.74 us
  transfers between devices with their start and end apart: 4, of which 4 were waited for; matrix products, arithmetic and copies ran while one was open for 0% of the time, Pallas kernels for 8%

profile of v2, /device:TPU:1, one launch (start us, length us, event | category | flops | bytes accessed | tf_op | source)
XLA Modules:
  0.0 96.0 jit_solution(14442325155756259765)
XLA Ops:
  0.6 0.0 copy-start.1
  0.6 1.3 %broadcast_in_dim.8 = s32[32,1,4]{2,1,0:T(1,128)} broadcast(s32[4]{0:T(128)} %bitcast.8), dimensions={2} | broadcast | bytes 528 | tf_op jit(solution)/shard_map/broadcast_in_dim | solution.py:448
  1.9 11.0 %all-to-all-start = ((s32[32,1,4]{2,1,0:T(1,128)}), s32[32,1,4]{2,1,0:T(1,128)S(1)}, u32[]{:S(2)}, u32[]{:S(2)}) async-start(s32[32,1,4]{2,1,0:T(1,128)} %broadcast_in_dim.8), calls=%async_computation | async-start | bytes 32768 | tf_op jit(solution)/shard_map/all_to_all | solution.py:446
  13.0 4.3 %strips.1 = bf16[8,64,512]{2,1,0:T(8,128)(2,1)} custom-call(bf16[2,2,64,8192]{3,2,1,0:T(8,128)(2,1)} %model_ref.1), custom_call_target="tpu_custom_call" | custom-call | flops 536870912 | bytes 5242880 | tf_op jit(solution)/shard_map/strips/pallas_call | solution.py:151
  17.2 0.0 copy-start
  17.2 3.5 %all-to-all-done = s32[32,1,4]{2,1,0:T(1,128)S(1)} async-done(((s32[32,1,4]{2,1,0:T(1,128)}), s32[32,1,4]{2,1,0:T(1,128)S(1)}, u32[]{:S(2)}, u32[]{:S(2)}) %all-to-all-start) | async-done | bytes 544 | tf_op jit(solution)/shard_map/all_to_all | solution.py:446
  20.7 6.4 %all-to-all-start.1 = ((bf16[8,64,512]{2,1,0:T(8,128)(2,1)}), bf16[8,64,512]{2,1,0:T(8,128)(2,1)S(1)}, u32[]{:S(2)}, u32[]{:S(2)}) async-start(bf16[8,64,512]{2,1,0:T(8,128)(2,1)} %strips.1), calls=%async_computation.1 | async-start | bytes 1048576 | tf_op jit(solution)/shard_map/all_to_all | solution.py:446
  27.7 1.2 %waves.1.d_ref = f32[2,4,128,128]{3,2,1,0:T(8,128)S(1)} custom-call(), custom_call_target="tpu_custom_call" | custom-call | flops 8388608 | bytes 1048576 | tf_op jit(solution)/shard_map/waves/pallas_call | solution.py:187
  28.9 0.0 copy-done.1
  28.9 2.4 %operator.1 = (bf16[1024,1024]{1,0:T(8,128)(2,1)S(1)}, f32[32,128]{1,0:T(8,128)S(1)}) custom-call(s32[32,4]{1,0:T(8,128)S(1)} %bitcast.5, s32[256]{0:T(256)S(1)} %copy-done.1, s32[1]{0:T(128)S(6)} %copy.15.count_ref, f32[2,4,128,128]{3,2,1,0:T(8,128)S(1)} %waves.1.d_ref), custom_call_target="tpu_custom_call" | custom-call | flops 20971520 | bytes 8388608 | tf_op jit(solution)/shard_map/operator/pallas_call | solution.py:233
  31.3 4.7 %all-to-all-done.1.strips_ref = bf16[8,64,512]{2,1,0:T(8,128)(2,1)S(1)} async-done(((bf16[8,64,512]{2,1,0:T(8,128)(2,1)}), bf16[8,64,512]{2,1,0:T(8,128)(2,1)S(1)}, u32[]{:S(2)}, u32[]{:S(2)}) %all-to-all-start.1) | async-done | bytes 524320 | tf_op jit(solution)/shard_map/all_to_all | solution.py:446
  36.1 2.3 %fore.1 = (bf16[16,32,256]{2,1,0:T(8,128)(2,1)S(1)}, bf16[16,32,256]{2,1,0:T(8,128)(2,1)S(1)}) custom-call(s32[32,4]{1,0:T(8,128)S(1)} %bitcast.6, s32[256]{0:T(256)S(1)} %copy-done.1, bf16[1024,1024]{1,0:T(8,128)(2,1)S(1)} %get-tuple-element.8.h_ref, bf16[8,64,512]{2,1,0:T(8,128)(2,1)S(1)} %all-to-all-done.1.strips_ref), custom_call_target="tpu_custom_call" | custom-call | flops 1073741824 | bytes 4194304 | tf_op jit(solution)/shard_map/fore/pallas_call | solution.py:265
  38.4 3.1 %collective-permute-start = (bf16[16,32,256]{2,1,0:T(8,128)(2,1)S(1)}, bf16[16,32,256]{2,1,0:T(8,128)(2,1)S(1)}, u32[]{:S(2)}, u32[]{:S(2)}) collective-permute-start(bf16[16,32,256]{2,1,0:T(8,128)(2,1)S(1)} %get-tuple-element.11), channel_id=1, source_target_pairs={{0,16},{16,0},{1,17},{17,1},{2,18},{18,2},{3,19},{19,3},{4,20},{20... | collective-permute-start | bytes 786440 | tf_op jit(solution)/shard_map/ppermute | solution.py:453
  41.5 1.2 %collective-permute-done.other_ref = bf16[16,32,256]{2,1,0:T(8,128)(2,1)S(1)} collective-permute-done((bf16[16,32,256]{2,1,0:T(8,128)(2,1)S(1)}, bf16[16,32,256]{2,1,0:T(8,128)(2,1)S(1)}, u32[]{:S(2)}, u32[]{:S(2)}) %collective-permute-start) | collective-permute-done | bytes 262176 | tf_op jit(solution)/shard_map/ppermute | solution.py:453
  42.7 0.1 add.1
  42.7 14.3 %all_to_all.28.parts_ref = bf16[16,32,256]{2,1,0:T(8,128)(2,1)S(1)} all-to-all(bf16[16,32,256]{2,1,0:T(8,128)(2,1)S(1)} %add.1), channel_id=1, replica_groups=mesh['zh'=4,'zl'=2,'core'=2,'xh'=2,'y'=4,'sub'=2] {'zh','zl','sub'}, dimensions={0} | all-to-all | bytes 524288 | tf_op jit(solution)/shard_map/all_to_all | solution.py:446
  57.0 0.0 copy-done
  57.0 1.3 %subgrid.1 = (bf16[4,32,8,256]{3,2,1,0:T(8,128)(2,1)}, bf16[16,32,256]{2,1,0:T(8,128)(2,1)S(1)}) custom-call(f32[32,128]{1,0:T(8,128)S(1)} %get-tuple-element.9.live_ref, bf16[16,32,256]{2,1,0:T(8,128)(2,1)S(1)} %all_to_all.28.parts_ref, bf16[4,32,8,256]{3,2,1,0:T(8,128)(2,1)S(1)} %bitcast.4), custom_call_target="tpu_custom_call" | custom-call | flops 20971520 | bytes 2097152 | tf_op jit(solution)/shard_map/subgrid/pallas_call | solution.py:347
  58.3 13.4 %all_to_all.29.own_ref = bf16[16,32,256]{2,1,0:T(8,128)(2,1)S(1)} all-to-all(bf16[16,32,256]{2,1,0:T(8,128)(2,1)S(1)} %get-tuple-element.12), channel_id=1, replica_groups=mesh['zh'=4,'zl'=2,'core'=2,'xh'=2,'y'=4,'sub'=2] {'zh','zl','sub'}, dimensions={0} | all-to-all | bytes 524288 | tf_op jit(solution)/shard_map/all_to_all | solution.py:446
  71.7 3.0 %collective-permute-start.1 = (bf16[16,32,256]{2,1,0:T(8,128)(2,1)S(1)}, bf16[16,32,256]{2,1,0:T(8,128)(2,1)S(1)}, u32[]{:S(2)}, u32[]{:S(2)}) collective-permute-start(bf16[16,32,256]{2,1,0:T(8,128)(2,1)S(1)} %all_to_all.29.own_ref), channel_id=1, source_target_pairs={{0,16},{16,0},{1,17},{17,1},{2,18},{18,2},{3,19},{19,3},{4,20},{20... | collective-permute-start | bytes 786440 | tf_op jit(solution)/shard_map/ppermute | solution.py:457
  74.6 1.2 %collective-permute-done.1.other_ref = bf16[16,32,256]{2,1,0:T(8,128)(2,1)S(1)} collective-permute-done((bf16[16,32,256]{2,1,0:T(8,128)(2,1)S(1)}, bf16[16,32,256]{2,1,0:T(8,128)(2,1)S(1)}, u32[]{:S(2)}, u32[]{:S(2)}) %collective-permute-start.1) | collective-permute-done | bytes 262176 | tf_op jit(solution)/shard_map/ppermute | solution.py:457
  75.8 2.7 %back.1 = bf16[8,64,512]{2,1,0:T(8,128)(2,1)S(1)} custom-call(s32[32,4]{1,0:T(8,128)S(1)} %bitcast.7, s32[256]{0:T(256)S(1)} %copy-done.1, bf16[1024,1024]{1,0:T(8,128)(2,1)S(1)} %get-tuple-element.8.h_ref, bf16[16,32,256]{2,1,0:T(8,128)(2,1)S(1)} %all_to_all.29.own_ref, bf16[16,32,256]{2,1,0:T(8,128)(2,1)S(1)} %collective-permute-done.1.other_ref), custom_call_target="tpu_custom_call" | custom-call | flops 1073741824 | bytes 4194304 | tf_op jit(solution)/shard_map/back/pallas_call | solution.py:384
  78.5 13.6 %all_to_all.30.parts_ref = bf16[8,64,512]{2,1,0:T(8,128)(2,1)S(1)} all-to-all(bf16[8,64,512]{2,1,0:T(8,128)(2,1)S(1)} %back.1), channel_id=1, replica_groups=mesh['zh'=4,'zl'=2,'core'=2,'xh'=2,'y'=4,'sub'=2] {'xh','y'}, dimensions={0} | all-to-all | bytes 1048576 | tf_op jit(solution)/shard_map/all_to_all | solution.py:446
  92.1 3.9 %facets.1 = bf16[2,2,64,8192]{3,2,1,0:T(8,128)(2,1)} custom-call(bf16[8,64,512]{2,1,0:T(8,128)(2,1)S(1)} %all_to_all.30.parts_ref), custom_call_target="tpu_custom_call" | custom-call | flops 536870912 | bytes 5242880 | tf_op jit(solution)/shard_map/facets/pallas_call | solution.py:424
Async XLA Ops:
  0.6 28.3 %copy-start.1 = (s32[256]{0:T(256)S(1)}, s32[256]{0:T(256)}, u32[]{:S(2)}) copy-start(s32[256]{0:T(256)} %offsets_ref.5) | copy-start | bytes 3076
  1.9 18.8 %all-to-all-start = ((s32[32,1,4]{2,1,0:T(1,128)}), s32[32,1,4]{2,1,0:T(1,128)S(1)}, u32[]{:S(2)}, u32[]{:S(2)}) async-start(s32[32,1,4]{2,1,0:T(1,128)} %broadcast_in_dim.8), calls=%async_computation | async-start | bytes 32768 | tf_op jit(solution)/shard_map/all_to_all | solution.py:446
  17.2 39.8 %copy-start = (bf16[1,4,32,8,256]{4,3,2,1,0:T(8,128)(2,1)S(1)}, bf16[1,4,32,8,256]{4,3,2,1,0:T(8,128)(2,1)}, u32[]{:S(2)}) copy-start(bf16[1,4,32,8,256]{4,3,2,1,0:T(8,128)(2,1)} %param.9) | copy-start | bytes 1572868
  20.7 15.3 %all-to-all-start.1 = ((bf16[8,64,512]{2,1,0:T(8,128)(2,1)}), bf16[8,64,512]{2,1,0:T(8,128)(2,1)S(1)}, u32[]{:S(2)}, u32[]{:S(2)}) async-start(bf16[8,64,512]{2,1,0:T(8,128)(2,1)} %strips.1), calls=%async_computation.1 | async-start | bytes 1048576 | tf_op jit(solution)/shard_map/all_to_all | solution.py:446
  38.4 4.3 %collective-permute-start = (bf16[16,32,256]{2,1,0:T(8,128)(2,1)S(1)}, bf16[16,32,256]{2,1,0:T(8,128)(2,1)S(1)}, u32[]{:S(2)}, u32[]{:S(2)}) collective-permute-start(bf16[16,32,256]{2,1,0:T(8,128)(2,1)S(1)} %get-tuple-element.11), channel_id=1, source_target_pairs={{0,16},{16,0},{1,17},{17,1},{2,18},{18,2},{3,19},{19,3},{4,20},{20... | collective-permute-start | bytes 786440 | tf_op jit(solution)/shard_map/ppermute | solution.py:453
  71.7 4.1 %collective-permute-start.1 = (bf16[16,32,256]{2,1,0:T(8,128)(2,1)S(1)}, bf16[16,32,256]{2,1,0:T(8,128)(2,1)S(1)}, u32[]{:S(2)}, u32[]{:S(2)}) collective-permute-start(bf16[16,32,256]{2,1,0:T(8,128)(2,1)S(1)} %all_to_all.29.own_ref), channel_id=1, source_target_pairs={{0,16},{16,0},{1,17},{17,1},{2,18},{18,2},{3,19},{19,3},{4,20},{20... | collective-permute-start | bytes 786440 | tf_op jit(solution)/shard_map/ppermute | solution.py:457

commit v3 on v2

--- a/solution.py
+++ b/solution.py
@@ -90,19 +90,15 @@
 def phase_table(ref):
     shape = (SG + TR, 2 * CS)
     cosine, sine = turn(iota(shape, 0) & (SG - 1), SG)
-    ref[0] = cosine
-    ref[1] = jnp.where(iota(shape, 1) < CS, -sine, sine)
-
-
-def phases(ref, tiles_ref, offsets_ref, first):
-    parts = [[], []]
-    for i in range(8):
-        index, s = subgrid_of(first + i)
-        for j in range(TM):
-            at = (tiles_ref[index, j] - 16 * offsets_ref[s]) & (SG - 1)
-            for c in range(2):
-                parts[c].append(ref[c, pl.ds(at, TR), :])
-    real, imag = (jnp.concatenate(x, axis=0) for x in parts)
+    ref[...] = jnp.where(iota(shape, 1) < CS, cosine, sine)
+
+
+def factors(ref, step):
+    x = ref[step * 8 * W : (step + 1) * 8 * W, :].astype(f32)
+    y = pltpu.roll(x, CS, 1)
+    left = iota(x.shape, 1) < CS
+    real = jnp.where(left, x, y)
+    imag = jnp.where(left, -y, x)
     return jnp.concatenate([real, real], axis=1), jnp.concatenate([imag, imag], axis=1)
 
 
@@ -194,7 +190,20 @@
     )()
 
 
-def operator_kernel(tiles_ref, offsets_ref, count_ref, d_ref, h_ref, live_ref, e_ref):
+def operator_kernel(
+    tiles_ref, offsets_ref, count_ref, d_ref, h_ref, live_ref, factor_ref, table_ref, e_ref, phase_ref, buffer, sems, base_ref
+):
+    def copy(i):
+        return pltpu.make_async_copy(buffer.at[i], table_ref.at[:, pl.ds(pl.multiple_of(i * QT, QT), QT)], sems.at[i])
+
+    def block(i, carry):
+        buffer[i] = column_block(base_ref, i)
+        copy(i).start()
+        return carry
+
+    column_start(base_ref)
+    lax.fori_loop(0, FP // QT, block, 0)
+    phase_table(phase_ref)
     live_ref[...] = jnp.where(iota((W, 128), 0) < TR * count_ref[0], 1.0, 0.0)
     place = line_rows((8, LP))
     line = iota((8, LP), 0)
@@ -202,21 +211,24 @@
 
     def body(step, carry):
         offset = jnp.zeros((8, LP), jnp.int32)
-        index = []
+        index, offs = [], []
         for i in range(8):
             at, s = subgrid_of(step * 8 + i)
             index.append(at)
+            offs.append(offsets_ref[s])
             offset = jnp.where(line == i, offsets_ref[s], offset)
         cosine, sine = turn((offset * place) & (SKY - 1), SKY)
         e_ref[0] = cosine * scale
         e_ref[1] = -sine * scale
         for half in range(2):
-            real, imag = [], []
+            real, imag, factor = [], [], []
             for i in range(4 * half, 4 * half + 4):
                 er = e_ref[0, i : i + 1, :]
                 ei = e_ref[1, i : i + 1, :]
                 for j in range(TM):
                     at = tiles_ref[index[i], j]
+                    n = (at - 16 * offs[i]) & (SG - 1)
+                    factor.append(phase_ref[pl.ds(n, TR), :])
                     dr = jnp.concatenate([d_ref[0, q, pl.ds(at, TR), :] for q in range(LP // 128)], axis=1)
                     di = jnp.concatenate([d_ref[1, q, pl.ds(at, TR), :] for q in range(LP // 128)], axis=1)
                     real.append(dr * er - di * ei)
@@ -224,26 +236,39 @@
             rows = pl.ds(pl.multiple_of(step * 8 * W + half * 4 * W, 4 * W), 4 * W)
             h_ref[rows, :LP] = jnp.concatenate(real, axis=0).astype(bf16)
             h_ref[rows, LP:] = jnp.concatenate(imag, axis=0).astype(bf16)
+            factor_ref[rows, :] = jnp.concatenate(factor, axis=0).astype(bf16)
         return carry
 
     lax.fori_loop(0, LS // 8, body, 0)
+    for i in range(FP // QT):
+        copy(i).wait()
 
 
 def operator_call(tiles, offsets, count, waves):
     return pl.pallas_call(
         operator_kernel,
         in_specs=[SMEM, SMEM, SMEM, VMEM],
-        out_specs=[VMEM, VMEM],
-        out_shape=[jax.ShapeDtypeStruct((LS * W, 2 * LP), bf16), jax.ShapeDtypeStruct((W, 128), f32)],
-        scratch_shapes=[pltpu.VMEM((2, 8, LP), f32)],
+        out_specs=[VMEM, VMEM, VMEM, HBM],
+        out_shape=[
+            jax.ShapeDtypeStruct((LS * W, 2 * LP), bf16),
+            jax.ShapeDtypeStruct((W, 128), f32),
+            jax.ShapeDtypeStruct((LS * W, 2 * CS), bf16),
+            pltpu.HBM((2 * CS, FP), bf16),
+        ],
+        scratch_shapes=[
+            pltpu.VMEM((2, 8, LP), f32),
+            pltpu.VMEM((SG + TR, 2 * CS), f32),
+            pltpu.VMEM((FP // QT, 2 * CS, QT), bf16),
+            pltpu.SemaphoreType.DMA((FP // QT,)),
+            pltpu.VMEM((6, 8, QT), f32),
+        ],
         compiler_params=params(24),
         cost_estimate=pl.CostEstimate(flops=20 << 20, bytes_accessed=8 << 20, transcendentals=0),
         name="operator",
     )(tiles, offsets, count, waves)
 
 
-def fore_kernel(tiles_ref, offsets_ref, h_ref, strips_ref, own_ref, other_ref, rhs_ref, phase_ref):
-    phase_table(phase_ref)
+def fore_kernel(factor_ref, h_ref, strips_ref, own_ref, other_ref, rhs_ref):
     left = iota((PB, 2 * CS), 1) < CS
     for r in range(ROWS):
         strips = strips_ref[r]
@@ -254,27 +279,24 @@
     rows = 8 * W
     for step in range(4):
         out = jnp.dot(h_ref[step * rows : (step + 1) * rows, :], rhs_ref[...], preferred_element_type=f32)
-        real, imag = phases(phase_ref, tiles_ref, offsets_ref, step * 8)
+        real, imag = factors(factor_ref, step)
         second = out[:, 4 * CS :]
         out = out[:, : 4 * CS] + second * real + swapped(second) * imag
         ref = own_ref if step < 2 else other_ref
         ref[step % 2 * 8 : step % 2 * 8 + 8] = out.reshape(8, W, 4 * CS).astype(bf16)
 
 
-def fore_call(tiles, offsets, h, strips):
+def fore_call(factor, h, strips):
     return pl.pallas_call(
         fore_kernel,
-        in_specs=[SMEM, SMEM, VMEM, VMEM],
+        in_specs=[VMEM, VMEM, VMEM],
         out_specs=[VMEM, VMEM],
         out_shape=[jax.ShapeDtypeStruct((LS // 2, W, 4 * CS), bf16)] * 2,
-        scratch_shapes=[
-            pltpu.VMEM((2 * LP, 8 * CS), bf16),
-            pltpu.VMEM((2, SG + TR, 2 * CS), f32),
-        ],
+        scratch_shapes=[pltpu.VMEM((2 * LP, 8 * CS), bf16)],
         compiler_params=params(24),
         cost_estimate=pl.CostEstimate(flops=1 << 30, bytes_accessed=4 << 20, transcendentals=0),
         name="fore",
-    )(tiles, offsets, h, strips)
+    )(factor, h, strips)
 
 
 def add_kernel(own_ref, other_ref, out_ref):
@@ -359,15 +381,14 @@
     )(live, parts, vis)
 
 
-def back_kernel(tiles_ref, offsets_ref, h_ref, own_ref, other_ref, out_ref, rhs_ref, phase_ref):
-    phase_table(phase_ref)
+def back_kernel(factor_ref, h_ref, own_ref, other_ref, out_ref, rhs_ref):
     total = LS * W
     left = (iota((8 * W, 8 * CS), 1) & (2 * CS - 1)) < CS
     for step in range(4):
         ref = own_ref if step < 2 else other_ref
         x = ref[step % 2 * 8 : step % 2 * 8 + 8].reshape(8 * W, 4 * CS).astype(f32)
         y = swapped(x)
-        real, imag = phases(phase_ref, tiles_ref, offsets_ref, step * 8)
+        real, imag = factors(factor_ref, step)
         both = jnp.concatenate([x, x * real - y * imag], axis=1)
         turned = jnp.concatenate([y, y * real + x * imag], axis=1)
         rhs_ref[step * 8 * W : (step + 1) * 8 * W, :] = both.astype(bf16)
@@ -380,22 +401,21 @@
         out_ref[step * 4 : step * 4 + 4] = out.reshape(4, PB, 8 * CS).astype(bf16)
 
 
-def back_call(tiles, offsets, h, own, other):
+def back_call(factor, h, own, other):
     return pl.pallas_call(
         back_kernel,
-        in_specs=[SMEM, SMEM, VMEM, VMEM, VMEM],
+        in_specs=[VMEM, VMEM, VMEM, VMEM],
         out_specs=VMEM,
         out_shape=jax.ShapeDtypeStruct((ROWS, PB, 8 * CS), bf16),
-        scratch_shapes=[pltpu.VMEM((2 * LS * W, 8 * CS), bf16), pltpu.VMEM((2, SG + TR, 2 * CS), f32)],
+        scratch_shapes=[pltpu.VMEM((2 * LS * W, 8 * CS), bf16)],
         compiler_params=params(24),
         cost_estimate=pl.CostEstimate(flops=1 << 30, bytes_accessed=4 << 20, transcendentals=0),
         name="back",
-    )(tiles, offsets, h, own, other)
-
-
-def facets_kernel(parts_ref, out_ref, buffer, sems, lhs_ref, base_ref):
+    )(factor, h, own, other)
+
+
+def facets_kernel(parts_ref, table_ref, out_ref, buffer, sems, lhs_ref):
     steps = FP // QT
-    column_start(base_ref)
     total = parts_ref[0].astype(f32)
     for r in range(1, ROWS):
         total = total + parts_ref[r].astype(f32)
@@ -409,7 +429,8 @@
         return pltpu.make_async_copy(buffer.at[i], out_ref.at[:, :, :, pl.ds(pl.multiple_of(i * QT, QT), QT)], sems.at[i])
 
     def body(i, carry):
-        out = jnp.dot(lhs_ref[...], column_block(base_ref, i), preferred_element_type=f32)
+        table = table_ref[:, pl.ds(pl.multiple_of(i * QT, QT), QT)]
+        out = jnp.dot(lhs_ref[...], table, preferred_element_type=f32)
         buffer[i] = out.reshape(2, 2, PB, QT).astype(bf16)
         copy(i).start()
         return carry
@@ -419,23 +440,22 @@
         copy(i).wait()
 
 
-def facets_call(parts):
+def facets_call(parts, table):
     steps = FP // QT
     return pl.pallas_call(
         facets_kernel,
-        in_specs=[VMEM],
+        in_specs=[VMEM, VMEM],
         out_specs=HBM,
         out_shape=jax.ShapeDtypeStruct((2, 2, PB, FP), bf16),
         scratch_shapes=[
             pltpu.VMEM((steps, 2, 2, PB, QT), bf16),
             pltpu.SemaphoreType.DMA((steps,)),
             pltpu.VMEM((4 * PB, 2 * CS), bf16),
-            pltpu.VMEM((6, 8, QT), f32),
         ],
         compiler_params=params(24),
         cost_estimate=pl.CostEstimate(flops=2 * 256 * 128 * FP, bytes_accessed=5 << 20, transcendentals=0),
         name="facets",
-    )(parts)
+    )(parts, table)
 
 
 def local(facet_model, sub_offsets, tile_rows, tile_counts, visibilities):
@@ -447,16 +467,16 @@
 
     tiles = exchange(jnp.broadcast_to(tile_rows, (LS, TM)), all_line)
     strips = exchange(strips_call(facet_model), rows_line)
-    h, live = operator_call(tiles, sub_offsets, tile_counts, waves_call())
-
-    own, other = fore_call(tiles, sub_offsets, h, strips)
+    h, live, factor, table = operator_call(tiles, sub_offsets, tile_counts, waves_call())
+
+    own, other = fore_call(factor, h, strips)
     other = lax.ppermute(other, "core", swap)
     parts = exchange(add_call(own, other), grid_line)
     residual, back = subgrid_call(live, parts, visibilities[0])
     own = exchange(back, grid_line)
     other = lax.ppermute(own, "core", swap)
-    sums = exchange(back_call(tiles, sub_offsets, h, own, other), rows_line)
-    return facets_call(sums), residual[None]
+    sums = exchange(back_call(factor, h, own, other), rows_line)
+    return facets_call(sums, table), residual[None]
 
 
 def solution(mesh):

time: 96.3 us -> 93.7 us (0.973)
  waiting for transfers between devices: 10.6 us -> 9.05 us
  Pallas kernels: 18.1 us -> 17 us
    pallas_call x3, Pallas kernels: 8.91 us -> 6.35 us  [the longest x1 3.23 us: facets_call(): pl.pallas_call(facets_kernel, in_specs=[VMEM, VMEM], out_specs=HBM, out_s...]
    all_to_all x2, waiting for transfers between devices: 8.23 us -> 6.73 us  [exchange(): return lax.all_to_all(x, axes, split_axis=0, concat_axis=0, tiled=True)]
    pallas_call x1, Pallas kernels: 2.38 us -> 3.87 us  [operator_call(): pl.pallas_call(operator_kernel, in_specs=[SMEM, SMEM, SMEM, VMEM], out_sp...]
  transfers between devices with their start and end apart: 4 -> 4, of which waited for: 4 -> 4; matrix products, arithmetic and copies ran while one was open for 0% -> 0% of each run, Pallas kernels for 8% -> 10%
where the time goes in v3:
time: 93.7 us; the launch traced here: 93.4 us
  blocking collectives  41.2 us (44%)
  starting transfers between devices  23.5 us (25%)
  Pallas kernels  17 us (18%)
  waiting for transfers between devices  9.05 us (10%)
  between operations  1.37 us (1%)
  local copies, waits for them, and re-layouts  1.29 us (1%)
    all_to_all x3, blocking collectives, exchange(): return lax.all_to_all(x, axes, split_axis=0, concat_axis=0, tiled=True)  41.2 us
    all_to_all x2, starting transfers between devices, exchange(): return lax.all_to_all(x, axes, split_axis=0, concat_axis=0, tiled=True)  17.4 us
    all_to_all x2, waiting for transfers between devices, exchange(): return lax.all_to_all(x, axes, split_axis=0, concat_axis=0, tiled=True)  6.73 us
    pallas_call x1, Pallas kernels, strips_call(): pl.pallas_call(strips_kernel, in_specs=[HBM], out_specs=VMEM, out_shape=j...  4.27 us
    pallas_call x1, Pallas kernels, operator_call(): pl.pallas_call(operator_kernel, in_specs=[SMEM, SMEM, SMEM, VMEM], out_sp...  3.87 us
    pallas_call x1, Pallas kernels, facets_call(): pl.pallas_call(facets_kernel, in_specs=[VMEM, VMEM], out_specs=HBM, out_s...  3.23 us
    ppermute x1, starting transfers between devices, local(): other = lax.ppermute(other, 'core', swap)  3.12 us
    ppermute x1, starting transfers between devices, local(): other = lax.ppermute(own, 'core', swap)  2.95 us
  transfers between devices with their start and end apart: 4, of which 4 were waited for; matrix products, arithmetic and copies ran while one was open for 0% of the time, Pallas kernels for 10%

profile of v3, /device:TPU:1, one launch (start us, length us, event | category | flops | bytes accessed | tf_op | source)
XLA Modules:
  0.0 93.4 jit_solution(10153885808304759938)
XLA Ops:
  0.6 0.0 copy-start.2
  0.6 1.3 %broadcast_in_dim.8 = s32[32,1,4]{2,1,0:T(1,128)} broadcast(s32[4]{0:T(128)} %bitcast.6), dimensions={2} | broadcast | bytes 528 | tf_op jit(solution)/shard_map/broadcast_in_dim | solution.py:468
  1.9 11.0 %all-to-all-start = ((s32[32,1,4]{2,1,0:T(1,128)}), s32[32,1,4]{2,1,0:T(1,128)S(1)}, u32[]{:S(2)}, u32[]{:S(2)}) async-start(s32[32,1,4]{2,1,0:T(1,128)} %broadcast_in_dim.8), calls=%async_computation | async-start | bytes 32768 | tf_op jit(solution)/shard_map/all_to_all | solution.py:466
  13.0 4.3 %strips.1 = bf16[8,64,512]{2,1,0:T(8,128)(2,1)} custom-call(bf16[2,2,64,8192]{3,2,1,0:T(8,128)(2,1)} %model_ref.1), custom_call_target="tpu_custom_call" | custom-call | flops 536870912 | bytes 5242880 | tf_op jit(solution)/shard_map/strips/pallas_call | solution.py:147
  17.2 0.0 copy-start.1
  17.2 3.5 %all-to-all-done = s32[32,1,4]{2,1,0:T(1,128)S(1)} async-done(((s32[32,1,4]{2,1,0:T(1,128)}), s32[32,1,4]{2,1,0:T(1,128)S(1)}, u32[]{:S(2)}, u32[]{:S(2)}) %all-to-all-start) | async-done | bytes 544 | tf_op jit(solution)/shard_map/all_to_all | solution.py:466
  20.7 6.4 %all-to-all-start.1 = ((bf16[8,64,512]{2,1,0:T(8,128)(2,1)}), bf16[8,64,512]{2,1,0:T(8,128)(2,1)S(1)}, u32[]{:S(2)}, u32[]{:S(2)}) async-start(bf16[8,64,512]{2,1,0:T(8,128)(2,1)} %strips.1), calls=%async_computation.1 | async-start | bytes 1048576 | tf_op jit(solution)/shard_map/all_to_all | solution.py:466
  27.7 1.2 %waves.1.d_ref = f32[2,4,128,128]{3,2,1,0:T(8,128)S(1)} custom-call(), custom_call_target="tpu_custom_call" | custom-call | flops 8388608 | bytes 1048576 | tf_op jit(solution)/shard_map/waves/pallas_call | solution.py:183
  28.9 0.0 copy-done.2
  28.9 3.9 %operator.1 = (bf16[1024,1024]{1,0:T(8,128)(2,1)S(1)}, f32[32,128]{1,0:T(8,128)S(1)}, bf16[1024,128]{1,0:T(8,128)(2,1)S(1)}, bf16[128,8192]{1,0:T(8,128)(2,1)}) custom-call(s32[32,4]{1,0:T(8,128)S(1)} %bitcast.5, s32[256]{0:T(256)S(1)} %copy-done.2, s32[1]{0:T(128)S(6)} %copy.11.count_ref, f32[2,4,128,128]{3,2,1,0:T(8,128)S(1)} %waves.1.d_ref), custom_call_target="tpu_custom_call" | custom-call | flops 20971520 | bytes 8388608 | tf_op jit(solution)/shard_map/operator/pallas_call | solution.py:248
  32.8 3.2 %all-to-all-done.1.strips_ref = bf16[8,64,512]{2,1,0:T(8,128)(2,1)S(1)} async-done(((bf16[8,64,512]{2,1,0:T(8,128)(2,1)}), bf16[8,64,512]{2,1,0:T(8,128)(2,1)S(1)}, u32[]{:S(2)}, u32[]{:S(2)}) %all-to-all-start.1) | async-done | bytes 524320 | tf_op jit(solution)/shard_map/all_to_all | solution.py:466
  36.1 1.4 %fore.1 = (bf16[16,32,256]{2,1,0:T(8,128)(2,1)S(1)}, bf16[16,32,256]{2,1,0:T(8,128)(2,1)S(1)}) custom-call(bf16[1024,128]{1,0:T(8,128)(2,1)S(1)} %get-tuple-element.10.factor_ref, bf16[1024,1024]{1,0:T(8,128)(2,1)S(1)} %get-tuple-element.11.h_ref, bf16[8,64,512]{2,1,0:T(8,128)(2,1)S(1)} %all-to-all-done.1.strips_ref), custom_call_target="tpu_custom_call" | custom-call | flops 1073741824 | bytes 4194304 | tf_op jit(solution)/shard_map/fore/pallas_call | solution.py:290
  37.5 0.0 copy-start
  37.5 3.1 %collective-permute-start = (bf16[16,32,256]{2,1,0:T(8,128)(2,1)S(1)}, bf16[16,32,256]{2,1,0:T(8,128)(2,1)S(1)}, u32[]{:S(2)}, u32[]{:S(2)}) collective-permute-start(bf16[16,32,256]{2,1,0:T(8,128)(2,1)S(1)} %get-tuple-element.14), channel_id=1, source_target_pairs={{0,16},{16,0},{1,17},{17,1},{2,18},{18,2},{3,19},{19,3},{4,20},{20... | collective-permute-start | bytes 786440 | tf_op jit(solution)/shard_map/ppermute | solution.py:473
  40.6 1.2 %collective-permute-done.other_ref = bf16[16,32,256]{2,1,0:T(8,128)(2,1)S(1)} collective-permute-done((bf16[16,32,256]{2,1,0:T(8,128)(2,1)S(1)}, bf16[16,32,256]{2,1,0:T(8,128)(2,1)S(1)}, u32[]{:S(2)}, u32[]{:S(2)}) %collective-permute-start) | collective-permute-done | bytes 262176 | tf_op jit(solution)/shard_map/ppermute | solution.py:473
  41.8 0.1 add.1
  41.8 14.3 %all_to_all.28.parts_ref = bf16[16,32,256]{2,1,0:T(8,128)(2,1)S(1)} all-to-all(bf16[16,32,256]{2,1,0:T(8,128)(2,1)S(1)} %add.1), channel_id=1, replica_groups=mesh['zh'=4,'zl'=2,'core'=2,'xh'=2,'y'=4,'sub'=2] {'zh','zl','sub'}, dimensions={0} | all-to-all | bytes 524288 | tf_op jit(solution)/shard_map/all_to_all | solution.py:466
  56.1 0.0 copy-done.1
  56.1 1.3 %subgrid.1 = (bf16[4,32,8,256]{3,2,1,0:T(8,128)(2,1)}, bf16[16,32,256]{2,1,0:T(8,128)(2,1)S(1)}) custom-call(f32[32,128]{1,0:T(8,128)S(1)} %get-tuple-element.12.live_ref, bf16[16,32,256]{2,1,0:T(8,128)(2,1)S(1)} %all_to_all.28.parts_ref, bf16[4,32,8,256]{3,2,1,0:T(8,128)(2,1)S(1)} %bitcast.4), custom_call_target="tpu_custom_call" | custom-call | flops 20971520 | bytes 2097152 | tf_op jit(solution)/shard_map/subgrid/pallas_call | solution.py:369
  57.4 13.4 %all_to_all.29.own_ref = bf16[16,32,256]{2,1,0:T(8,128)(2,1)S(1)} all-to-all(bf16[16,32,256]{2,1,0:T(8,128)(2,1)S(1)} %get-tuple-element.15), channel_id=1, replica_groups=mesh['zh'=4,'zl'=2,'core'=2,'xh'=2,'y'=4,'sub'=2] {'zh','zl','sub'}, dimensions={0} | all-to-all | bytes 524288 | tf_op jit(solution)/shard_map/all_to_all | solution.py:466
  70.8 3.0 %collective-permute-start.1 = (bf16[16,32,256]{2,1,0:T(8,128)(2,1)S(1)}, bf16[16,32,256]{2,1,0:T(8,128)(2,1)S(1)}, u32[]{:S(2)}, u32[]{:S(2)}) collective-permute-start(bf16[16,32,256]{2,1,0:T(8,128)(2,1)S(1)} %all_to_all.29.own_ref), channel_id=1, source_target_pairs={{0,16},{16,0},{1,17},{17,1},{2,18},{18,2},{3,19},{19,3},{4,20},{20... | collective-permute-start | bytes 786440 | tf_op jit(solution)/shard_map/ppermute | solution.py:477
  73.7 1.2 %collective-permute-done.1.other_ref = bf16[16,32,256]{2,1,0:T(8,128)(2,1)S(1)} collective-permute-done((bf16[16,32,256]{2,1,0:T(8,128)(2,1)S(1)}, bf16[16,32,256]{2,1,0:T(8,128)(2,1)S(1)}, u32[]{:S(2)}, u32[]{:S(2)}) %collective-permute-start.1) | collective-permute-done | bytes 262176 | tf_op jit(solution)/shard_map/ppermute | solution.py:477
  74.9 1.7 %back.1 = bf16[8,64,512]{2,1,0:T(8,128)(2,1)S(1)} custom-call(bf16[1024,128]{1,0:T(8,128)(2,1)S(1)} %get-tuple-element.10.factor_ref, bf16[1024,1024]{1,0:T(8,128)(2,1)S(1)} %get-tuple-element.11.h_ref, bf16[16,32,256]{2,1,0:T(8,128)(2,1)S(1)} %all_to_all.29.own_ref, bf16[16,32,256]{2,1,0:T(8,128)(2,1)S(1)} %collective-permute-done.1.other_ref), custom_call_target="tpu_custom_call" | custom-call | flops 1073741824 | bytes 4194304 | tf_op jit(solution)/shard_map/back/pallas_call | solution.py:405
  76.6 13.5 %all_to_all.30.parts_ref = bf16[8,64,512]{2,1,0:T(8,128)(2,1)S(1)} all-to-all(bf16[8,64,512]{2,1,0:T(8,128)(2,1)S(1)} %back.1), channel_id=1, replica_groups=mesh['zh'=4,'zl'=2,'core'=2,'xh'=2,'y'=4,'sub'=2] {'xh','y'}, dimensions={0} | all-to-all | bytes 1048576 | tf_op jit(solution)/shard_map/all_to_all | solution.py:466
  90.2 0.0 copy-done
  90.2 3.2 %facets.1 = bf16[2,2,64,8192]{3,2,1,0:T(8,128)(2,1)} custom-call(bf16[8,64,512]{2,1,0:T(8,128)(2,1)S(1)} %all_to_all.30.parts_ref, bf16[128,8192]{1,0:T(8,128)(2,1)S(1)} %copy-done), custom_call_target="tpu_custom_call" | custom-call | flops 536870912 | bytes 5242880 | tf_op jit(solution)/shard_map/facets/pallas_call | solution.py:445
Async XLA Ops:
  0.6 28.3 %copy-start.2 = (s32[256]{0:T(256)S(1)}, s32[256]{0:T(256)}, u32[]{:S(2)}) copy-start(s32[256]{0:T(256)} %offsets_ref.1) | copy-start | bytes 3076
  1.9 18.8 %all-to-all-start = ((s32[32,1,4]{2,1,0:T(1,128)}), s32[32,1,4]{2,1,0:T(1,128)S(1)}, u32[]{:S(2)}, u32[]{:S(2)}) async-start(s32[32,1,4]{2,1,0:T(1,128)} %broadcast_in_dim.8), calls=%async_computation | async-start | bytes 32768 | tf_op jit(solution)/shard_map/all_to_all | solution.py:466
  17.2 38.9 %copy-start.1 = (bf16[1,4,32,8,256]{4,3,2,1,0:T(8,128)(2,1)S(1)}, bf16[1,4,32,8,256]{4,3,2,1,0:T(8,128)(2,1)}, u32[]{:S(2)}) copy-start(bf16[1,4,32,8,256]{4,3,2,1,0:T(8,128)(2,1)} %param.9) | copy-start | bytes 1572868
  20.7 15.3 %all-to-all-start.1 = ((bf16[8,64,512]{2,1,0:T(8,128)(2,1)}), bf16[8,64,512]{2,1,0:T(8,128)(2,1)S(1)}, u32[]{:S(2)}, u32[]{:S(2)}) async-start(bf16[8,64,512]{2,1,0:T(8,128)(2,1)} %strips.1), calls=%async_computation.1 | async-start | bytes 1048576 | tf_op jit(solution)/shard_map/all_to_all | solution.py:466
  37.5 52.7 %copy-start = (bf16[128,8192]{1,0:T(8,128)(2,1)S(1)}, bf16[128,8192]{1,0:T(8,128)(2,1)}, u32[]{:S(2)}) copy-start(bf16[128,8192]{1,0:T(8,128)(2,1)} %get-tuple-element.16.table_ref) | copy-start | bytes 6291460
  37.5 4.3 %collective-permute-start = (bf16[16,32,256]{2,1,0:T(8,128)(2,1)S(1)}, bf16[16,32,256]{2,1,0:T(8,128)(2,1)S(1)}, u32[]{:S(2)}, u32[]{:S(2)}) collective-permute-start(bf16[16,32,256]{2,1,0:T(8,128)(2,1)S(1)} %get-tuple-element.14), channel_id=1, source_target_pairs={{0,16},{16,0},{1,17},{17,1},{2,18},{18,2},{3,19},{19,3},{4,20},{20... | collective-permute-start | bytes 786440 | tf_op jit(solution)/shard_map/ppermute | solution.py:473
  70.8 4.1 %collective-permute-start.1 = (bf16[16,32,256]{2,1,0:T(8,128)(2,1)S(1)}, bf16[16,32,256]{2,1,0:T(8,128)(2,1)S(1)}, u32[]{:S(2)}, u32[]{:S(2)}) collective-permute-start(bf16[16,32,256]{2,1,0:T(8,128)(2,1)S(1)} %all_to_all.29.own_ref), channel_id=1, source_target_pairs={{0,16},{16,0},{1,17},{17,1},{2,18},{18,2},{3,19},{19,3},{4,20},{20... | collective-permute-start | bytes 786440 | tf_op jit(solution)/shard_map/ppermute | solution.py:477

commit v4 on v3

--- a/solution.py
+++ b/solution.py
@@ -268,7 +268,21 @@
     )(tiles, offsets, count, waves)
 
 
-def fore_kernel(factor_ref, h_ref, strips_ref, own_ref, other_ref, rhs_ref):
+HALF = jax.ShapeDtypeStruct((LS // 2, W, 4 * CS), bf16)
+
+
+def fore_half(factor_ref, h_ref, rhs_ref, o, put):
+    rows = 8 * W
+    for q in range(2):
+        step = 2 * o + q
+        out = jnp.dot(h_ref[step * rows : (step + 1) * rows, :], rhs_ref[...], preferred_element_type=f32)
+        real, imag = factors(factor_ref, step)
+        second = out[:, 4 * CS :]
+        out = out[:, : 4 * CS] + second * real + swapped(second) * imag
+        put(slice(q * 8, q * 8 + 8), out.reshape(8, W, 4 * CS))
+
+
+def fore_other_kernel(factor_ref, h_ref, strips_ref, out_ref, rhs_ref):
     left = iota((PB, 2 * CS), 1) < CS
     for r in range(ROWS):
         strips = strips_ref[r]
@@ -276,27 +290,42 @@
         for at in range(0, 8 * CS, 2 * CS):
             turned = pltpu.roll(strips[:, at : at + 2 * CS].astype(f32), CS, 1)
             rhs_ref[LP + r * PB : LP + (r + 1) * PB, at : at + 2 * CS] = jnp.where(left, -turned, turned).astype(bf16)
-    rows = 8 * W
-    for step in range(4):
-        out = jnp.dot(h_ref[step * rows : (step + 1) * rows, :], rhs_ref[...], preferred_element_type=f32)
-        real, imag = factors(factor_ref, step)
-        second = out[:, 4 * CS :]
-        out = out[:, : 4 * CS] + second * real + swapped(second) * imag
-        ref = own_ref if step < 2 else other_ref
-        ref[step % 2 * 8 : step % 2 * 8 + 8] = out.reshape(8, W, 4 * CS).astype(bf16)
-
-
-def fore_call(factor, h, strips):
-    return pl.pallas_call(
-        fore_kernel,
+
+    def put(at, out):
+        out_ref[at] = out.astype(bf16)
+
+    fore_half(factor_ref, h_ref, rhs_ref, 1, put)
+
+
+def fore_own_kernel(factor_ref, h_ref, rhs_ref, out_ref):
+    def put(at, out):
+        out_ref[at] = out.astype(bf16)
+
+    fore_half(factor_ref, h_ref, rhs_ref, 0, put)
+
+
+def fore_other_call(factor, h, strips):
+    return pl.pallas_call(
+        fore_other_kernel,
         in_specs=[VMEM, VMEM, VMEM],
         out_specs=[VMEM, VMEM],
-        out_shape=[jax.ShapeDtypeStruct((LS // 2, W, 4 * CS), bf16)] * 2,
-        scratch_shapes=[pltpu.VMEM((2 * LP, 8 * CS), bf16)],
-        compiler_params=params(24),
-        cost_estimate=pl.CostEstimate(flops=1 << 30, bytes_accessed=4 << 20, transcendentals=0),
-        name="fore",
+        out_shape=[HALF, jax.ShapeDtypeStruct((2 * LP, 8 * CS), bf16)],
+        compiler_params=params(24),
+        cost_estimate=pl.CostEstimate(flops=1 << 29, bytes_accessed=4 << 20, transcendentals=0),
+        name="fore_other",
     )(factor, h, strips)
+
+
+def fore_own_call(factor, h, rhs):
+    return pl.pallas_call(
+        fore_own_kernel,
+        in_specs=[VMEM, VMEM, VMEM],
+        out_specs=VMEM,
+        out_shape=HALF,
+        compiler_params=params(24),
+        cost_estimate=pl.CostEstimate(flops=1 << 29, bytes_accessed=4 << 20, transcendentals=0),
+        name="fore_own",
+    )(factor, h, rhs)
 
 
 def add_kernel(own_ref, other_ref, out_ref):
@@ -381,37 +410,51 @@
     )(live, parts, vis)
 
 
-def back_kernel(factor_ref, h_ref, own_ref, other_ref, out_ref, rhs_ref):
-    total = LS * W
+def back_half(factor_ref, h_ref, x_ref, rhs_ref, o, put):
     left = (iota((8 * W, 8 * CS), 1) & (2 * CS - 1)) < CS
-    for step in range(4):
-        ref = own_ref if step < 2 else other_ref
-        x = ref[step % 2 * 8 : step % 2 * 8 + 8].reshape(8 * W, 4 * CS).astype(f32)
+    total = LS * W // 2
+    for q in range(2):
+        x = x_ref[q * 8 : q * 8 + 8].reshape(8 * W, 4 * CS).astype(f32)
         y = swapped(x)
-        real, imag = factors(factor_ref, step)
+        real, imag = factors(factor_ref, 2 * o + q)
         both = jnp.concatenate([x, x * real - y * imag], axis=1)
         turned = jnp.concatenate([y, y * real + x * imag], axis=1)
-        rhs_ref[step * 8 * W : (step + 1) * 8 * W, :] = both.astype(bf16)
-        rhs_ref[total + step * 8 * W : total + (step + 1) * 8 * W, :] = jnp.where(left, turned, -turned).astype(bf16)
+        rhs_ref[q * 8 * W : (q + 1) * 8 * W, :] = both.astype(bf16)
+        rhs_ref[total + q * 8 * W : total + (q + 1) * 8 * W, :] = jnp.where(left, turned, -turned).astype(bf16)
     dims = (((0,), (0,)), ((), ()))
+    rows = slice(o * total, (o + 1) * total)
     for step in range(2):
         at = step * 4 * PB
-        out = lax.dot_general(h_ref[:, at : at + 4 * PB], rhs_ref[:total], dims, preferred_element_type=f32)
-        out = out + lax.dot_general(h_ref[:, LP + at : LP + at + 4 * PB], rhs_ref[total:], dims, preferred_element_type=f32)
-        out_ref[step * 4 : step * 4 + 4] = out.reshape(4, PB, 8 * CS).astype(bf16)
-
-
-def back_call(factor, h, own, other):
-    return pl.pallas_call(
-        back_kernel,
-        in_specs=[VMEM, VMEM, VMEM, VMEM],
+        out = lax.dot_general(h_ref[rows, at : at + 4 * PB], rhs_ref[:total], dims, preferred_element_type=f32)
+        out = out + lax.dot_general(h_ref[rows, LP + at : LP + at + 4 * PB], rhs_ref[total:], dims, preferred_element_type=f32)
+        put(slice(step * 4, step * 4 + 4), out.reshape(4, PB, 8 * CS))
+
+
+def back_own_kernel(factor_ref, h_ref, x_ref, out_ref, rhs_ref):
+    def put(at, out):
+        out_ref[at] = out
+
+    back_half(factor_ref, h_ref, x_ref, rhs_ref, 0, put)
+
+
+def back_other_kernel(factor_ref, h_ref, x_ref, own_ref, out_ref, rhs_ref):
+    def put(at, out):
+        out_ref[at] = (own_ref[at] + out).astype(bf16)
+
+    back_half(factor_ref, h_ref, x_ref, rhs_ref, 1, put)
+
+
+def back_call(kernel, name, dtype, *args):
+    return pl.pallas_call(
+        kernel,
+        in_specs=[VMEM] * len(args),
         out_specs=VMEM,
-        out_shape=jax.ShapeDtypeStruct((ROWS, PB, 8 * CS), bf16),
-        scratch_shapes=[pltpu.VMEM((2 * LS * W, 8 * CS), bf16)],
-        compiler_params=params(24),
-        cost_estimate=pl.CostEstimate(flops=1 << 30, bytes_accessed=4 << 20, transcendentals=0),
-        name="back",
-    )(factor, h, own, other)
+        out_shape=jax.ShapeDtypeStruct((ROWS, PB, 8 * CS), dtype),
+        scratch_shapes=[pltpu.VMEM((LS * W, 8 * CS), bf16)],
+        compiler_params=params(24),
+        cost_estimate=pl.CostEstimate(flops=1 << 29, bytes_accessed=4 << 20, transcendentals=0),
+        name=name,
+    )(*args)
 
 
 def facets_kernel(parts_ref, table_ref, out_ref, buffer, sems, lhs_ref):
@@ -469,13 +512,15 @@
     strips = exchange(strips_call(facet_model), rows_line)
     h, live, factor, table = operator_call(tiles, sub_offsets, tile_counts, waves_call())
 
-    own, other = fore_call(factor, h, strips)
+    other, rhs = fore_other_call(factor, h, strips)
     other = lax.ppermute(other, "core", swap)
+    own = fore_own_call(factor, h, rhs)
     parts = exchange(add_call(own, other), grid_line)
     residual, back = subgrid_call(live, parts, visibilities[0])
     own = exchange(back, grid_line)
     other = lax.ppermute(own, "core", swap)
-    sums = exchange(back_call(factor, h, own, other), rows_line)
+    sums = back_call(back_own_kernel, "back_own", f32, factor, h, own)
+    sums = exchange(back_call(back_other_kernel, "back_other", bf16, factor, h, other, sums), rows_line)
     return facets_call(sums, table), residual[None]
 
 

time: 93.7 us -> 92.3 us (0.985)
  waiting for transfers between devices: 9.05 us -> 7.3 us
    ppermute x1, waiting for transfers between devices: 1.16 us -> 0.19 us  [local(): other = lax.ppermute(own, 'core', swap)]
    pallas_call x2 -> x4, Pallas kernels: 3.12 us -> 3.54 us  [the longest x2 1.93 us: back_call(): pl.pallas_call(kernel, in_specs=[VMEM] * len(args), out_specs=VMEM, out_s...]
  transfers between devices with their start and end apart: 4 -> 4, of which waited for: 4 -> 4; matrix products, arithmetic and copies ran while one was open for 0% -> 0% of each run, Pallas kernels for 10% -> 12%
where the time goes in v4:
time: 92.3 us; the launch traced here: 91.9 us
  blocking collectives  41.1 us (45%)
  starting transfers between devices  23.5 us (25%)
  Pallas kernels  17.4 us (19%)
  waiting for transfers between devices  7.3 us (8%)
  between operations  1.38 us (1%)
  local copies, waits for them, and re-layouts  1.29 us (1%)
    all_to_all x3, blocking collectives, exchange(): return lax.all_to_all(x, axes, split_axis=0, concat_axis=0, tiled=True)  41.1 us
    all_to_all x2, starting transfers between devices, exchange(): return lax.all_to_all(x, axes, split_axis=0, concat_axis=0, tiled=True)  17.4 us
    all_to_all x2, waiting for transfers between devices, exchange(): return lax.all_to_all(x, axes, split_axis=0, concat_axis=0, tiled=True)  6.73 us
    pallas_call x1, Pallas kernels, strips_call(): pl.pallas_call(strips_kernel, in_specs=[HBM], out_specs=VMEM, out_shape=j...  4.27 us
    pallas_call x1, Pallas kernels, operator_call(): pl.pallas_call(operator_kernel, in_specs=[SMEM, SMEM, SMEM, VMEM], out_sp...  3.87 us
    pallas_call x1, Pallas kernels, facets_call(): pl.pallas_call(facets_kernel, in_specs=[VMEM, VMEM], out_specs=HBM, out_s...  3.22 us
    ppermute x1, starting transfers between devices, local(): other = lax.ppermute(other, 'core', swap)  3.12 us
    ppermute x1, starting transfers between devices, local(): other = lax.ppermute(own, 'core', swap)  2.95 us
  transfers between devices with their start and end apart: 4, of which 4 were waited for; matrix products, arithmetic and copies ran while one was open for 0% of the time, Pallas kernels for 12%

profile of v4, /device:TPU:1, one launch (start us, length us, event | category | flops | bytes accessed | tf_op | source)
XLA Modules:
  0.0 91.9 jit_solution(7793017606972594703)
XLA Ops:
  0.6 0.0 copy-start.2
  0.6 1.3 %broadcast_in_dim.8 = s32[32,1,4]{2,1,0:T(1,128)} broadcast(s32[4]{0:T(128)} %bitcast.6), dimensions={2} | broadcast | bytes 528 | tf_op jit(solution)/shard_map/broadcast_in_dim | solution.py:511
  1.9 11.0 %all-to-all-start = ((s32[32,1,4]{2,1,0:T(1,128)}), s32[32,1,4]{2,1,0:T(1,128)S(1)}, u32[]{:S(2)}, u32[]{:S(2)}) async-start(s32[32,1,4]{2,1,0:T(1,128)} %broadcast_in_dim.8), calls=%async_computation | async-start | bytes 32768 | tf_op jit(solution)/shard_map/all_to_all | solution.py:509
  13.0 4.3 %strips.1 = bf16[8,64,512]{2,1,0:T(8,128)(2,1)} custom-call(bf16[2,2,64,8192]{3,2,1,0:T(8,128)(2,1)} %model_ref.1), custom_call_target="tpu_custom_call" | custom-call | flops 536870912 | bytes 5242880 | tf_op jit(solution)/shard_map/strips/pallas_call | solution.py:147
  17.2 3.5 %all-to-all-done = s32[32,1,4]{2,1,0:T(1,128)S(1)} async-done(((s32[32,1,4]{2,1,0:T(1,128)}), s32[32,1,4]{2,1,0:T(1,128)S(1)}, u32[]{:S(2)}, u32[]{:S(2)}) %all-to-all-start) | async-done | bytes 544 | tf_op jit(solution)/shard_map/all_to_all | solution.py:509
  20.7 6.4 %all-to-all-start.1 = ((bf16[8,64,512]{2,1,0:T(8,128)(2,1)}), bf16[8,64,512]{2,1,0:T(8,128)(2,1)S(1)}, u32[]{:S(2)}, u32[]{:S(2)}) async-start(bf16[8,64,512]{2,1,0:T(8,128)(2,1)} %strips.1), calls=%async_computation.1 | async-start | bytes 1048576 | tf_op jit(solution)/shard_map/all_to_all | solution.py:509
  27.7 1.2 %waves.1.d_ref = f32[2,4,128,128]{3,2,1,0:T(8,128)S(1)} custom-call(), custom_call_target="tpu_custom_call" | custom-call | flops 8388608 | bytes 1048576 | tf_op jit(solution)/shard_map/waves/pallas_call | solution.py:183
  28.9 0.0 copy-done.2
  28.9 0.0 copy-start.1
  29.0 3.9 %operator.1 = (bf16[1024,1024]{1,0:T(8,128)(2,1)S(1)}, f32[32,128]{1,0:T(8,128)S(1)}, bf16[1024,128]{1,0:T(8,128)(2,1)S(1)}, bf16[128,8192]{1,0:T(8,128)(2,1)}) custom-call(s32[32,4]{1,0:T(8,128)S(1)} %bitcast.5, s32[256]{0:T(256)S(1)} %copy-done.2, s32[1]{0:T(128)S(6)} %copy.11.count_ref, f32[2,4,128,128]{3,2,1,0:T(8,128)S(1)} %waves.1.d_ref), custom_call_target="tpu_custom_call" | custom-call | flops 20971520 | bytes 8388608 | tf_op jit(solution)/shard_map/operator/pallas_call | solution.py:248
  32.8 3.2 %all-to-all-done.1.strips_ref = bf16[8,64,512]{2,1,0:T(8,128)(2,1)S(1)} async-done(((bf16[8,64,512]{2,1,0:T(8,128)(2,1)}), bf16[8,64,512]{2,1,0:T(8,128)(2,1)S(1)}, u32[]{:S(2)}, u32[]{:S(2)}) %all-to-all-start.1) | async-done | bytes 524320 | tf_op jit(solution)/shard_map/all_to_all | solution.py:509
  36.1 0.8 fore_other.1
  36.9 3.1 %collective-permute-start = (bf16[16,32,256]{2,1,0:T(8,128)(2,1)S(1)}, bf16[16,32,256]{2,1,0:T(8,128)(2,1)S(1)}, u32[]{:S(2)}, u32[]{:S(2)}) collective-permute-start(bf16[16,32,256]{2,1,0:T(8,128)(2,1)S(1)} %get-tuple-element.14), channel_id=1, source_target_pairs={{0,16},{16,0},{1,17},{17,1},{2,18},{18,2},{3,19},{19,3},{4,20},{20... | collective-permute-start | bytes 786440 | tf_op jit(solution)/shard_map/ppermute | solution.py:516
  40.0 0.8 fore_own.1.own_ref
  40.8 0.4 collective-permute-done.other_ref
  41.2 0.1 add.1
  41.3 14.1 %all_to_all.28.parts_ref = bf16[16,32,256]{2,1,0:T(8,128)(2,1)S(1)} all-to-all(bf16[16,32,256]{2,1,0:T(8,128)(2,1)S(1)} %add.1), channel_id=1, replica_groups=mesh['zh'=4,'zl'=2,'core'=2,'xh'=2,'y'=4,'sub'=2] {'zh','zl','sub'}, dimensions={0} | all-to-all | bytes 524288 | tf_op jit(solution)/shard_map/all_to_all | solution.py:509
  55.4 0.0 copy-done.1
  55.4 1.3 %subgrid.1 = (bf16[4,32,8,256]{3,2,1,0:T(8,128)(2,1)}, bf16[16,32,256]{2,1,0:T(8,128)(2,1)S(1)}) custom-call(f32[32,128]{1,0:T(8,128)S(1)} %get-tuple-element.12.live_ref, bf16[16,32,256]{2,1,0:T(8,128)(2,1)S(1)} %all_to_all.28.parts_ref, bf16[4,32,8,256]{3,2,1,0:T(8,128)(2,1)S(1)} %bitcast.4), custom_call_target="tpu_custom_call" | custom-call | flops 20971520 | bytes 2097152 | tf_op jit(solution)/shard_map/subgrid/pallas_call | solution.py:398
  56.7 13.4 %all_to_all.29.x_ref = bf16[16,32,256]{2,1,0:T(8,128)(2,1)S(1)} all-to-all(bf16[16,32,256]{2,1,0:T(8,128)(2,1)S(1)} %get-tuple-element.15), channel_id=1, replica_groups=mesh['zh'=4,'zl'=2,'core'=2,'xh'=2,'y'=4,'sub'=2] {'zh','zl','sub'}, dimensions={0} | all-to-all | bytes 524288 | tf_op jit(solution)/shard_map/all_to_all | solution.py:509
  70.1 0.0 copy-start
  70.1 3.0 %collective-permute-start.1 = (bf16[16,32,256]{2,1,0:T(8,128)(2,1)S(1)}, bf16[16,32,256]{2,1,0:T(8,128)(2,1)S(1)}, u32[]{:S(2)}, u32[]{:S(2)}) collective-permute-start(bf16[16,32,256]{2,1,0:T(8,128)(2,1)S(1)} %all_to_all.29.x_ref), channel_id=1, source_target_pairs={{0,16},{16,0},{1,17},{17,1},{2,18},{18,2},{3,19},{19,3},{4,20},{20... | collective-permute-start | bytes 786440 | tf_op jit(solution)/shard_map/ppermute | solution.py:521
  73.0 1.0 %back_own.1.own_ref = f32[8,64,512]{2,1,0:T(8,128)S(1)} custom-call(bf16[1024,128]{1,0:T(8,128)(2,1)S(1)} %get-tuple-element.10.factor_ref, bf16[1024,1024]{1,0:T(8,128)(2,1)S(1)} %get-tuple-element.11.h_ref, bf16[16,32,256]{2,1,0:T(8,128)(2,1)S(1)} %all_to_all.29.x_ref), custom_call_target="tpu_custom_call" | custom-call | flops 536870912 | bytes 4194304 | tf_op jit(solution)/shard_map/back_own/pallas_call | solution.py:448
  74.0 0.2 collective-permute-done.1.x_ref
  74.2 1.0 %back_other.1 = bf16[8,64,512]{2,1,0:T(8,128)(2,1)S(1)} custom-call(bf16[1024,128]{1,0:T(8,128)(2,1)S(1)} %get-tuple-element.10.factor_ref, bf16[1024,1024]{1,0:T(8,128)(2,1)S(1)} %get-tuple-element.11.h_ref, bf16[16,32,256]{2,1,0:T(8,128)(2,1)S(1)} %collective-permute-done.1.x_ref, f32[8,64,512]{2,1,0:T(8,128)S(1)} %back_own.1.own_ref), custom_call_target="tpu_custom_call" | custom-call | flops 536870912 | bytes 4194304 | tf_op jit(solution)/shard_map/back_other/pallas_call | solution.py:448
  75.2 13.5 %all_to_all.30.parts_ref = bf16[8,64,512]{2,1,0:T(8,128)(2,1)S(1)} all-to-all(bf16[8,64,512]{2,1,0:T(8,128)(2,1)S(1)} %back_other.1), channel_id=1, replica_groups=mesh['zh'=4,'zl'=2,'core'=2,'xh'=2,'y'=4,'sub'=2] {'xh','y'}, dimensions={0} | all-to-all | bytes 1048576 | tf_op jit(solution)/shard_map/all_to_all | solution.py:509
  88.7 0.0 copy-done
  88.7 3.2 %facets.1 = bf16[2,2,64,8192]{3,2,1,0:T(8,128)(2,1)} custom-call(bf16[8,64,512]{2,1,0:T(8,128)(2,1)S(1)} %all_to_all.30.parts_ref, bf16[128,8192]{1,0:T(8,128)(2,1)S(1)} %copy-done), custom_call_target="tpu_custom_call" | custom-call | flops 536870912 | bytes 5242880 | tf_op jit(solution)/shard_map/facets/pallas_call | solution.py:488
Async XLA Ops:
  0.6 28.3 %copy-start.2 = (s32[256]{0:T(256)S(1)}, s32[256]{0:T(256)}, u32[]{:S(2)}) copy-start(s32[256]{0:T(256)} %offsets_ref.1) | copy-start | bytes 3076
  1.9 18.8 %all-to-all-start = ((s32[32,1,4]{2,1,0:T(1,128)}), s32[32,1,4]{2,1,0:T(1,128)S(1)}, u32[]{:S(2)}, u32[]{:S(2)}) async-start(s32[32,1,4]{2,1,0:T(1,128)} %broadcast_in_dim.8), calls=%async_computation | async-start | bytes 32768 | tf_op jit(solution)/shard_map/all_to_all | solution.py:509
  20.7 15.3 %all-to-all-start.1 = ((bf16[8,64,512]{2,1,0:T(8,128)(2,1)}), bf16[8,64,512]{2,1,0:T(8,128)(2,1)S(1)}, u32[]{:S(2)}, u32[]{:S(2)}) async-start(bf16[8,64,512]{2,1,0:T(8,128)(2,1)} %strips.1), calls=%async_computation.1 | async-start | bytes 1048576 | tf_op jit(solution)/shard_map/all_to_all | solution.py:509
  28.9 26.5 %copy-start.1 = (bf16[1,4,32,8,256]{4,3,2,1,0:T(8,128)(2,1)S(1)}, bf16[1,4,32,8,256]{4,3,2,1,0:T(8,128)(2,1)}, u32[]{:S(2)}) copy-start(bf16[1,4,32,8,256]{4,3,2,1,0:T(8,128)(2,1)} %param.9) | copy-start | bytes 1572868
  36.9 4.3 %collective-permute-start = (bf16[16,32,256]{2,1,0:T(8,128)(2,1)S(1)}, bf16[16,32,256]{2,1,0:T(8,128)(2,1)S(1)}, u32[]{:S(2)}, u32[]{:S(2)}) collective-permute-start(bf16[16,32,256]{2,1,0:T(8,128)(2,1)S(1)} %get-tuple-element.14), channel_id=1, source_target_pairs={{0,16},{16,0},{1,17},{17,1},{2,18},{18,2},{3,19},{19,3},{4,20},{20... | collective-permute-start | bytes 786440 | tf_op jit(solution)/shard_map/ppermute | solution.py:516
  70.1 18.6 %copy-start = (bf16[128,8192]{1,0:T(8,128)(2,1)S(1)}, bf16[128,8192]{1,0:T(8,128)(2,1)}, u32[]{:S(2)}) copy-start(bf16[128,8192]{1,0:T(8,128)(2,1)} %get-tuple-element.16.table_ref) | copy-start | bytes 6291460
  70.1 4.1 %collective-permute-start.1 = (bf16[16,32,256]{2,1,0:T(8,128)(2,1)S(1)}, bf16[16,32,256]{2,1,0:T(8,128)(2,1)S(1)}, u32[]{:S(2)}, u32[]{:S(2)}) collective-permute-start(bf16[16,32,256]{2,1,0:T(8,128)(2,1)S(1)} %all_to_all.29.x_ref), channel_id=1, source_target_pairs={{0,16},{16,0},{1,17},{17,1},{2,18},{18,2},{3,19},{19,3},{4,20},{20... | collective-permute-start | bytes 786440 | tf_op jit(solution)/shard_map/ppermute | solution.py:521

commit v5 on v4

--- a/solution.py
+++ b/solution.py
@@ -161,6 +161,19 @@
     )(model)
 
 
+def grid_table():
+    l = iota((2 * CS, SG), 0) & (CS - 1)
+    upper = iota((2 * CS, SG), 0) < CS
+    v = iota((2 * CS, SG), 1)
+    rows = []
+    for b in range(2):
+        cosine, sine = turn((v * (2 * l + b)) & (SG - 1), SG)
+        real = jnp.where(upper, cosine, -sine)
+        imag = jnp.where(upper, sine, cosine)
+        rows.append(jnp.concatenate([real, imag], axis=1))
+    return (jnp.concatenate(rows, axis=0) * (1.0 / math.sqrt(SG))).astype(bf16)
+
+
 def waves_kernel(d_ref):
     p = line_rows((TR, LP))
     line = iota((TR, LP), 0)
@@ -191,7 +204,7 @@
 
 
 def operator_kernel(
-    tiles_ref, offsets_ref, count_ref, d_ref, h_ref, live_ref, factor_ref, table_ref, e_ref, phase_ref, buffer, sems, base_ref
+    tiles_ref, offsets_ref, count_ref, d_ref, h_ref, live_ref, factor_ref, grid_ref, table_ref, e_ref, phase_ref, buffer, sems, base_ref
 ):
     def copy(i):
         return pltpu.make_async_copy(buffer.at[i], table_ref.at[:, pl.ds(pl.multiple_of(i * QT, QT), QT)], sems.at[i])
@@ -204,6 +217,7 @@
     column_start(base_ref)
     lax.fori_loop(0, FP // QT, block, 0)
     phase_table(phase_ref)
+    grid_ref[...] = grid_table()
     live_ref[...] = jnp.where(iota((W, 128), 0) < TR * count_ref[0], 1.0, 0.0)
     place = line_rows((8, LP))
     line = iota((8, LP), 0)
@@ -248,11 +262,12 @@
     return pl.pallas_call(
         operator_kernel,
         in_specs=[SMEM, SMEM, SMEM, VMEM],
-        out_specs=[VMEM, VMEM, VMEM, HBM],
+        out_specs=[VMEM, VMEM, VMEM, VMEM, HBM],
         out_shape=[
             jax.ShapeDtypeStruct((LS * W, 2 * LP), bf16),
             jax.ShapeDtypeStruct((W, 128), f32),
             jax.ShapeDtypeStruct((LS * W, 2 * CS), bf16),
+            jax.ShapeDtypeStruct((4 * CS, 2 * SG), bf16),
             pltpu.HBM((2 * CS, FP), bf16),
         ],
         scratch_shapes=[
@@ -344,18 +359,8 @@
     )(own, other)
 
 
-def subgrid_kernel(live_ref, parts_ref, vis_ref, res_ref, out_ref, buffer, sems):
-    l = iota((2 * CS, SG), 0) & (CS - 1)
-    upper = iota((2 * CS, SG), 0) < CS
-    v = iota((2 * CS, SG), 1)
-    rows = []
-    for b in range(2):
-        cosine, sine = turn((v * (2 * l + b)) & (SG - 1), SG)
-        real = jnp.where(upper, cosine, -sine)
-        imag = jnp.where(upper, sine, cosine)
-        rows.append(jnp.concatenate([real, imag], axis=1))
-    table = (jnp.concatenate(rows, axis=0) * (1.0 / math.sqrt(SG))).astype(bf16)
-
+def subgrid_kernel(live_ref, grid_ref, parts_ref, vis_ref, res_ref, out_ref, buffer, sems):
+    table = grid_ref[...]
     fronts = []
     for b in range(2):
         total = parts_ref[b].astype(f32)
@@ -394,10 +399,10 @@
         pltpu.make_async_copy(buffer.at[j], res_ref.at[j], sems.at[j]).wait()
 
 
-def subgrid_call(live, parts, vis):
+def subgrid_call(live, grid, parts, vis):
     return pl.pallas_call(
         subgrid_kernel,
-        in_specs=[VMEM, VMEM, VMEM],
+        in_specs=[VMEM, VMEM, VMEM, VMEM],
         out_specs=[HBM, VMEM],
         out_shape=[
             jax.ShapeDtypeStruct((TM, CH, TR, 2 * SG), bf16),
@@ -407,7 +412,7 @@
         compiler_params=params(24),
         cost_estimate=pl.CostEstimate(flops=20 << 20, bytes_accessed=2 << 20, transcendentals=0),
         name="subgrid",
-    )(live, parts, vis)
+    )(live, grid, parts, vis)
 
 
 def back_half(factor_ref, h_ref, x_ref, rhs_ref, o, put):
@@ -510,13 +515,13 @@
 
     tiles = exchange(jnp.broadcast_to(tile_rows, (LS, TM)), all_line)
     strips = exchange(strips_call(facet_model), rows_line)
-    h, live, factor, table = operator_call(tiles, sub_offsets, tile_counts, waves_call())
+    h, live, factor, grid, table = operator_call(tiles, sub_offsets, tile_counts, waves_call())
 
     other, rhs = fore_other_call(factor, h, strips)
     other = lax.ppermute(other, "core", swap)
     own = fore_own_call(factor, h, rhs)
     parts = exchange(add_call(own, other), grid_line)
-    residual, back = subgrid_call(live, parts, visibilities[0])
+    residual, back = subgrid_call(live, grid, parts, visibilities[0])
     own = exchange(back, grid_line)
     other = lax.ppermute(own, "core", swap)
     sums = back_call(back_own_kernel, "back_own", f32, factor, h, own)

time: 92.3 us -> 92.1 us (level)
  waiting for transfers between devices: 7.3 us -> 5.84 us
  local copies, waits for them, and re-layouts: 1.29 us -> 2.55 us
    all_to_all x2, waiting for transfers between devices: 6.73 us -> 5.27 us  [exchange(): return lax.all_to_all(x, axes, split_axis=0, concat_axis=0, tiled=True)]
    unnamed x6 -> x10, local copies, waits for them, and re-layouts: 0.01 us -> 1.28 us
where the time goes in v5:
time: 92.1 us; the launch traced here: 91.7 us
  blocking collectives  41.1 us (45%)
  starting transfers between devices  23.5 us (26%)
  Pallas kernels  17.4 us (19%)
  waiting for transfers between devices  5.84 us (6%)
  local copies, waits for them, and re-layouts  2.55 us (3%)
  between operations  1.37 us (1%)
    all_to_all x3, blocking collectives, exchange(): return lax.all_to_all(x, axes, split_axis=0, concat_axis=0, tiled=True)  41.1 us
    all_to_all x2, starting transfers between devices, exchange(): return lax.all_to_all(x, axes, split_axis=0, concat_axis=0, tiled=True)  17.4 us
    all_to_all x2, waiting for transfers between devices, exchange(): return lax.all_to_all(x, axes, split_axis=0, concat_axis=0, tiled=True)  5.27 us
    pallas_call x1, Pallas kernels, strips_call(): pl.pallas_call(strips_kernel, in_specs=[HBM], out_specs=VMEM, out_shape=j...  4.27 us
    pallas_call x1, Pallas kernels, operator_call(): pl.pallas_call(operator_kernel, in_specs=[SMEM, SMEM, SMEM, VMEM], out_sp...  4.06 us
    pallas_call x1, Pallas kernels, facets_call(): pl.pallas_call(facets_kernel, in_specs=[VMEM, VMEM], out_specs=HBM, out_s...  3.22 us
    ppermute x1, starting transfers between devices, local(): other = lax.ppermute(other, 'core', swap)  3.12 us
    ppermute x1, starting transfers between devices, local(): other = lax.ppermute(own, 'core', swap)  2.95 us
  transfers between devices with their start and end apart: 4, of which 4 were waited for; matrix products, arithmetic and copies ran while one was open for 0% of the time, Pallas kernels for 12%

profile of v5, /device:TPU:1, one launch (start us, length us, event | category | flops | bytes accessed | tf_op | source)
XLA Modules:
  0.0 91.7 jit_solution(9234248308701557245)
XLA Ops:
  0.6 1.3 %broadcast_in_dim.8 = s32[32,1,4]{2,1,0:T(1,128)} broadcast(s32[4]{0:T(128)} %bitcast.6), dimensions={2} | broadcast | bytes 528 | tf_op jit(solution)/shard_map/broadcast_in_dim | solution.py:516
  1.9 11.0 %all-to-all-start = ((s32[32,1,4]{2,1,0:T(1,128)}), s32[32,1,4]{2,1,0:T(1,128)S(1)}, u32[]{:S(2)}, u32[]{:S(2)}) async-start(s32[32,1,4]{2,1,0:T(1,128)} %broadcast_in_dim.8), calls=%async_computation | async-start | bytes 32768 | tf_op jit(solution)/shard_map/all_to_all | solution.py:514
  12.9 4.3 %strips.1 = bf16[8,64,512]{2,1,0:T(8,128)(2,1)} custom-call(bf16[2,2,64,8192]{3,2,1,0:T(8,128)(2,1)} %model_ref.1), custom_call_target="tpu_custom_call" | custom-call | flops 536870912 | bytes 5242880 | tf_op jit(solution)/shard_map/strips/pallas_call | solution.py:147
  17.2 3.5 %all-to-all-done = s32[32,1,4]{2,1,0:T(1,128)S(1)} async-done(((s32[32,1,4]{2,1,0:T(1,128)}), s32[32,1,4]{2,1,0:T(1,128)S(1)}, u32[]{:S(2)}, u32[]{:S(2)}) %all-to-all-start) | async-done | bytes 544 | tf_op jit(solution)/shard_map/all_to_all | solution.py:514
  20.7 6.4 %all-to-all-start.1 = ((bf16[8,64,512]{2,1,0:T(8,128)(2,1)}), bf16[8,64,512]{2,1,0:T(8,128)(2,1)S(1)}, u32[]{:S(2)}, u32[]{:S(2)}) async-start(bf16[8,64,512]{2,1,0:T(8,128)(2,1)} %strips.1), calls=%async_computation.1 | async-start | bytes 1048576 | tf_op jit(solution)/shard_map/all_to_all | solution.py:514
  27.7 1.2 %waves.1.d_ref = f32[2,4,128,128]{3,2,1,0:T(8,128)S(1)} custom-call(), custom_call_target="tpu_custom_call" | custom-call | flops 8388608 | bytes 1048576 | tf_op jit(solution)/shard_map/waves/pallas_call | solution.py:196
  28.9 0.0 copy-start.4
  28.9 0.7 copy-done.4
  29.6 0.0 copy-start.1
  29.6 4.1 %operator.1 = (bf16[1024,1024]{1,0:T(8,128)(2,1)S(1)}, f32[32,128]{1,0:T(8,128)S(1)}, bf16[1024,128]{1,0:T(8,128)(2,1)S(1)}, bf16[256,256]{1,0:T(8,128)(2,1)S(1)}, bf16[128,8192]{1,0:T(8,128)(2,1)}) custom-call(s32[32,4]{1,0:T(8,128)S(1)} %bitcast.5, s32[256]{0:T(256)S(1)} %copy-done.4, s32[1]{0:T(128)S(6)} %copy.11.count_ref, f32[2,4,128,128]{3,2,1,0:T(8,128)S(1)} %waves.1.d_ref), custom_call_target="tpu_custom_call" | custom-call | flops 20971520 | bytes 8388608 | tf_op jit(solution)/shard_map/operator/pallas_call | solution.py:262
  33.7 0.0 copy-start.2
  33.7 0.6 copy-done.2
  34.3 1.8 %all-to-all-done.1.strips_ref = bf16[8,64,512]{2,1,0:T(8,128)(2,1)S(1)} async-done(((bf16[8,64,512]{2,1,0:T(8,128)(2,1)}), bf16[8,64,512]{2,1,0:T(8,128)(2,1)S(1)}, u32[]{:S(2)}, u32[]{:S(2)}) %all-to-all-start.1) | async-done | bytes 524320 | tf_op jit(solution)/shard_map/all_to_all | solution.py:514
  36.1 0.0 copy-start.3
  36.1 0.8 fore_other.1
  36.9 3.1 %collective-permute-start = (bf16[16,32,256]{2,1,0:T(8,128)(2,1)S(1)}, bf16[16,32,256]{2,1,0:T(8,128)(2,1)S(1)}, u32[]{:S(2)}, u32[]{:S(2)}) collective-permute-start(bf16[16,32,256]{2,1,0:T(8,128)(2,1)S(1)} %get-tuple-element.16), channel_id=1, source_target_pairs={{0,16},{16,0},{1,17},{17,1},{2,18},{18,2},{3,19},{19,3},{4,20},{20... | collective-permute-start | bytes 786440 | tf_op jit(solution)/shard_map/ppermute | solution.py:521
  40.0 0.8 fore_own.1.own_ref
  40.8 0.4 collective-permute-done.other_ref
  41.2 0.1 add.1
  41.3 14.1 %all_to_all.28.parts_ref = bf16[16,32,256]{2,1,0:T(8,128)(2,1)S(1)} all-to-all(bf16[16,32,256]{2,1,0:T(8,128)(2,1)S(1)} %add.1), channel_id=1, replica_groups=mesh['zh'=4,'zl'=2,'core'=2,'xh'=2,'y'=4,'sub'=2] {'zh','zl','sub'}, dimensions={0} | all-to-all | bytes 524288 | tf_op jit(solution)/shard_map/all_to_all | solution.py:514
  55.4 0.0 copy-done.1
  55.4 0.0 copy-done.3
  55.4 1.1 %subgrid.1 = (bf16[4,32,8,256]{3,2,1,0:T(8,128)(2,1)}, bf16[16,32,256]{2,1,0:T(8,128)(2,1)S(1)}) custom-call(f32[32,128]{1,0:T(8,128)S(1)} %copy-done.3, bf16[256,256]{1,0:T(8,128)(2,1)S(1)} %get-tuple-element.14.grid_ref, bf16[16,32,256]{2,1,0:T(8,128)(2,1)S(1)} %all_to_all.28.parts_ref, bf16[4,32,8,256]{3,2,1,0:T(8,128)(2,1)S(1)} %bitcast.4), custom_call_target="tpu_custom_call" | custom-call | flops 20971520 | bytes 2097152 | tf_op jit(solution)/shard_map/subgrid/pallas_call | solution.py:403
  56.5 13.4 %all_to_all.29.x_ref = bf16[16,32,256]{2,1,0:T(8,128)(2,1)S(1)} all-to-all(bf16[16,32,256]{2,1,0:T(8,128)(2,1)S(1)} %get-tuple-element.17), channel_id=1, replica_groups=mesh['zh'=4,'zl'=2,'core'=2,'xh'=2,'y'=4,'sub'=2] {'zh','zl','sub'}, dimensions={0} | all-to-all | bytes 524288 | tf_op jit(solution)/shard_map/all_to_all | solution.py:514
  69.9 0.0 copy-start
  69.9 3.0 %collective-permute-start.1 = (bf16[16,32,256]{2,1,0:T(8,128)(2,1)S(1)}, bf16[16,32,256]{2,1,0:T(8,128)(2,1)S(1)}, u32[]{:S(2)}, u32[]{:S(2)}) collective-permute-start(bf16[16,32,256]{2,1,0:T(8,128)(2,1)S(1)} %all_to_all.29.x_ref), channel_id=1, source_target_pairs={{0,16},{16,0},{1,17},{17,1},{2,18},{18,2},{3,19},{19,3},{4,20},{20... | collective-permute-start | bytes 786440 | tf_op jit(solution)/shard_map/ppermute | solution.py:526
  72.8 1.0 %back_own.1.own_ref = f32[8,64,512]{2,1,0:T(8,128)S(1)} custom-call(bf16[1024,128]{1,0:T(8,128)(2,1)S(1)} %get-tuple-element.11.factor_ref, bf16[1024,1024]{1,0:T(8,128)(2,1)S(1)} %get-tuple-element.12.h_ref, bf16[16,32,256]{2,1,0:T(8,128)(2,1)S(1)} %all_to_all.29.x_ref), custom_call_target="tpu_custom_call" | custom-call | flops 536870912 | bytes 4194304 | tf_op jit(solution)/shard_map/back_own/pallas_call | solution.py:453
  73.8 0.2 collective-permute-done.1.x_ref
  74.0 1.0 %back_other.1 = bf16[8,64,512]{2,1,0:T(8,128)(2,1)S(1)} custom-call(bf16[1024,128]{1,0:T(8,128)(2,1)S(1)} %get-tuple-element.11.factor_ref, bf16[1024,1024]{1,0:T(8,128)(2,1)S(1)} %get-tuple-element.12.h_ref, bf16[16,32,256]{2,1,0:T(8,128)(2,1)S(1)} %collective-permute-done.1.x_ref, f32[8,64,512]{2,1,0:T(8,128)S(1)} %back_own.1.own_ref), custom_call_target="tpu_custom_call" | custom-call | flops 536870912 | bytes 4194304 | tf_op jit(solution)/shard_map/back_other/pallas_call | solution.py:453
  75.0 13.6 %all_to_all.30.parts_ref = bf16[8,64,512]{2,1,0:T(8,128)(2,1)S(1)} all-to-all(bf16[8,64,512]{2,1,0:T(8,128)(2,1)S(1)} %back_other.1), channel_id=1, replica_groups=mesh['zh'=4,'zl'=2,'core'=2,'xh'=2,'y'=4,'sub'=2] {'xh','y'}, dimensions={0} | all-to-all | bytes 1048576 | tf_op jit(solution)/shard_map/all_to_all | solution.py:514
  88.5 0.0 copy-done
  88.5 3.2 %facets.1 = bf16[2,2,64,8192]{3,2,1,0:T(8,128)(2,1)} custom-call(bf16[8,64,512]{2,1,0:T(8,128)(2,1)S(1)} %all_to_all.30.parts_ref, bf16[128,8192]{1,0:T(8,128)(2,1)S(1)} %copy-done), custom_call_target="tpu_custom_call" | custom-call | flops 536870912 | bytes 5242880 | tf_op jit(solution)/shard_map/facets/pallas_call | solution.py:493
Async XLA Ops:
  1.9 18.8 %all-to-all-start = ((s32[32,1,4]{2,1,0:T(1,128)}), s32[32,1,4]{2,1,0:T(1,128)S(1)}, u32[]{:S(2)}, u32[]{:S(2)}) async-start(s32[32,1,4]{2,1,0:T(1,128)} %broadcast_in_dim.8), calls=%async_computation | async-start | bytes 32768 | tf_op jit(solution)/shard_map/all_to_all | solution.py:514
  20.7 15.3 %all-to-all-start.1 = ((bf16[8,64,512]{2,1,0:T(8,128)(2,1)}), bf16[8,64,512]{2,1,0:T(8,128)(2,1)S(1)}, u32[]{:S(2)}, u32[]{:S(2)}) async-start(bf16[8,64,512]{2,1,0:T(8,128)(2,1)} %strips.1), calls=%async_computation.1 | async-start | bytes 1048576 | tf_op jit(solution)/shard_map/all_to_all | solution.py:514
  28.9 0.7 copy-start.4
  29.6 25.8 %copy-start.1 = (bf16[1,4,32,8,256]{4,3,2,1,0:T(8,128)(2,1)S(1)}, bf16[1,4,32,8,256]{4,3,2,1,0:T(8,128)(2,1)}, u32[]{:S(2)}) copy-start(bf16[1,4,32,8,256]{4,3,2,1,0:T(8,128)(2,1)} %param.9) | copy-start | bytes 1572868
  33.7 0.6 copy-start.2
  36.1 19.3 %copy-start.3 = (f32[32,128]{1,0:T(8,128)S(1)}, f32[32,128]{1,0:T(8,128)}, u32[]{:S(2)}) copy-start(f32[32,128]{1,0:T(8,128)} %copy-done.2) | copy-start | bytes 49156
  36.9 4.3 %collective-permute-start = (bf16[16,32,256]{2,1,0:T(8,128)(2,1)S(1)}, bf16[16,32,256]{2,1,0:T(8,128)(2,1)S(1)}, u32[]{:S(2)}, u32[]{:S(2)}) collective-permute-start(bf16[16,32,256]{2,1,0:T(8,128)(2,1)S(1)} %get-tuple-element.16), channel_id=1, source_target_pairs={{0,16},{16,0},{1,17},{17,1},{2,18},{18,2},{3,19},{19,3},{4,20},{20... | collective-permute-start | bytes 786440 | tf_op jit(solution)/shard_map/ppermute | solution.py:521
  69.9 18.6 %copy-start = (bf16[128,8192]{1,0:T(8,128)(2,1)S(1)}, bf16[128,8192]{1,0:T(8,128)(2,1)}, u32[]{:S(2)}) copy-start(bf16[128,8192]{1,0:T(8,128)(2,1)} %get-tuple-element.18.table_ref) | copy-start | bytes 6291460
  69.9 4.1 %collective-permute-start.1 = (bf16[16,32,256]{2,1,0:T(8,128)(2,1)S(1)}, bf16[16,32,256]{2,1,0:T(8,128)(2,1)S(1)}, u32[]{:S(2)}, u32[]{:S(2)}) collective-permute-start(bf16[16,32,256]{2,1,0:T(8,128)(2,1)S(1)} %all_to_all.29.x_ref), channel_id=1, source_target_pairs={{0,16},{16,0},{1,17},{17,1},{2,18},{18,2},{3,19},{19,3},{4,20},{20... | collective-permute-start | bytes 786440 | tf_op jit(solution)/shard_map/ppermute | solution.py:526
